TPU v7x, 256 devices: a whole 4x4x8 slice. The times are simulated.
256 devices in a mesh: member: 8 (over z_lo, core), section: 4 (over x), atoms: 8 (over y, z_hi).
Axes of the slice: x: 4, y: 4, z: 8 (z_hi: 2, z_lo: 4; z = z_hi * 4 + z_lo), core: 2. Of those that a mesh axis runs over, the one named last changes fastest.
Arguments:
- positions: float32 [8, 3, 1024], P(None, None, 'atoms'), may hold values from -8 to 8
- atom_types: int32 [8, 1024], P(None, 'atoms'), may hold values from 0 to 127
- neighbors: int32 [8, 1024, 128], P(None, 'atoms'), may hold values from 0 to 1023
- nbr_mask: int32 [8, 1024, 128], P(None, 'atoms'), may hold values 0 or 1
- type_table: bfloat16 [8, 128, 128], P('member'), may hold values from -6 to 6
- norm_gain: bfloat16 [8, 4, 128], P('member', 'section'), may hold values from 0.25 to 1.75
- proj_weight: bfloat16 [8, 4, 128, 384], P('member', 'section'), may hold values from -0.5 to 0.5
- out_weight: bfloat16 [8, 4, 128, 128], P('member', 'section'), may hold values from -0.5 to 0.5
- force_coef: bfloat16 [8, 4, 4], P('member', 'section'), may hold values from -48 to 48
Outputs:
- atom_dev: float32 [8, 1024], P('section', 'atoms')
- max_dev: float32 [8], P('section')
- mean_force: float32 [8, 3, 1024], P('section', None, 'atoms')
Inputs may be any that keep to these rules, and one draw needn't show every extreme that they name: `neighbors`: indices of atoms of the same frame, repeats and the atom itself allowed.
All inputs are finite; a program needn't handle non-finite values. No bound on the sum of `nbr_mask` on one device may be relied on, other than what follows from the above.
Results may differ from a plain program's by a relative error of at most 0.013.
Values may be sent and summed in bfloat16 or wider, within the bound.
A program may use at most 64 MiB of HBM per device.

v0:
```python
import math

import jax
import jax.numpy as jnp
from jax import lax
from jax.sharding import PartitionSpec as P


def sent_to_all(x, axis):
    devices = lax.axis_size(axis)
    return lax.all_to_all(jnp.broadcast_to(x[None], (devices, *x.shape)), axis, 0, 0, tiled=True)


def joined_along(pieces, dim):
    pieces = jnp.moveaxis(pieces, 0, dim)
    dims = pieces.shape
    return pieces.reshape(*dims[:dim], dims[dim] * dims[dim + 1], *dims[dim + 2 :])


def gathered_copies(x, axis, dim):
    pieces = sent_to_all(x, axis)
    return joined_along(pieces, dim)


def side_by_side(arrays, axis, dim, along):
    widths = [math.prod(a.shape[along:]) for a in arrays]
    both = jnp.concatenate(
        [a.reshape(*a.shape[:along], w) for a, w in zip(arrays, widths)], axis=along
    )
    whole = lax.all_gather(both, axis, axis=dim, tiled=True)
    pieces = jnp.split(whole, [sum(widths[:k]) for k in range(1, len(widths))], axis=along)
    return tuple(
        (b.reshape(*whole.shape[:along], *a.shape[along:]) for a, b in zip(arrays, pieces))
    )


def of_everyone(x, axis):
    everything = sent_to_all(x, axis)
    return jnp.sum(everything, axis=0)


def in_one(arrays, axis):
    line, at, done = (jnp.concatenate([a.reshape(-1) for a in arrays]), 0, [])
    so_far = of_everyone(line, axis)
    for a in arrays:
        done.append(so_far[at : at + a.size].reshape(a.shape))
        at += a.size
    return tuple(done)


def of_everyone_2(x, axis):
    return sent_to_all(x, axis).max(axis=0)


def geometry(nbr, mask, pos_all, pos_own):
    total_atoms = pos_all.shape[1]
    hit = (nbr[:, :, None] == lax.iota(jnp.int32, total_atoms)[None, None, :]).astype(jnp.float32)
    counts = jnp.sum(hit * mask.astype(jnp.float32)[:, :, None], 1)
    delta = pos_all[:, None, :] - pos_own[:, :, None]
    switch = 1.0 / (1.0 + 0.125 * jnp.sum(delta * delta, 0))
    return (counts * switch, delta)


def block_dev(h_in, gain, proj, outw, coef, pair, delta, slots):
    width = h_in.shape[1]
    heads = coef.shape[0]
    head_dim = width // heads
    count = h_in.shape[0]
    hf = h_in.astype(jnp.float32)
    normed = (
        hf * lax.rsqrt(jnp.mean(hf * hf, -1, keepdims=True) + 1e-06) * gain.astype(jnp.float32)
    ).astype(jnp.bfloat16)
    query = jnp.dot(normed, proj[:, :width], preferred_element_type=jnp.float32).astype(
        jnp.bfloat16
    )
    keyval = jnp.dot(
        gathered_copies(normed, "atoms", 0), proj[:, width:], preferred_element_type=jnp.float32
    ).astype(jnp.bfloat16)
    total_atoms = keyval.shape[0]
    query3 = query.reshape(count, heads, head_dim)
    keys = keyval[:, :width].reshape(total_atoms, heads, head_dim)
    values = keyval[:, width:].reshape(total_atoms, heads, head_dim)
    scores = jnp.einsum(
        "ahd,jhd->haj", query3, keys, preferred_element_type=jnp.float32
    ) / math.sqrt(head_dim)
    weights = jax.nn.sigmoid(scores) * pair[None]
    message = jnp.einsum(
        "haj,jhd->ahd", weights.astype(jnp.bfloat16), values, preferred_element_type=jnp.float32
    )
    message = (message / slots).reshape(count, width).astype(jnp.bfloat16)
    h_out = (hf + jnp.dot(message, outw, preferred_element_type=jnp.float32)).astype(jnp.bfloat16)
    pair_coef = jnp.einsum("h,haj->aj", coef.astype(jnp.float32), weights)
    force = jnp.einsum("aj,caj->ca", pair_coef, delta) / slots
    return (h_out, force)


def embed(types_now, table):
    onehot = (types_now[:, None] == lax.iota(jnp.int32, table.shape[0])[None, :]).astype(
        jnp.bfloat16
    )
    return jnp.dot(onehot, table, preferred_element_type=jnp.float32).astype(jnp.bfloat16)


def shards(
    positions,
    atom_types,
    neighbors,
    nbr_mask,
    type_table,
    norm_gain,
    proj_weight,
    out_weight,
    force_coef,
):
    n_section = lax.axis_size("section")
    section_idx = lax.axis_index("section")
    frames = atom_types.shape[0]
    per_section = frames // n_section
    count = atom_types.shape[1]
    slots = neighbors.shape[2]
    table = type_table[0]
    pos_all = gathered_copies(positions, "atoms", 2)
    gains, projs, outs, coefs = side_by_side(
        (norm_gain, proj_weight, out_weight, force_coef), "section", 1, 2
    )
    first = section_idx * per_section

    def whole_frame(local, own_forces):
        frame = first + local
        nbr = lax.dynamic_index_in_dim(neighbors, frame, 0, keepdims=False)
        mask = lax.dynamic_index_in_dim(nbr_mask, frame, 0, keepdims=False)
        pos_now = lax.dynamic_index_in_dim(pos_all, frame, 0, keepdims=False)
        pos_own = lax.dynamic_index_in_dim(positions, frame, 0, keepdims=False)
        pair, delta = geometry(nbr, mask, pos_now, pos_own)
        h_cur = embed(lax.dynamic_index_in_dim(atom_types, frame, 0, keepdims=False), table)
        total = jnp.zeros((3, count), jnp.float32)
        for blk in range(n_section):
            h_cur, term = block_dev(
                h_cur, gains[0, blk], projs[0, blk], outs[0, blk], coefs[0, blk], pair, delta, slots
            )
            total = total + term
        return lax.dynamic_update_index_in_dim(own_forces, total, local, 0)

    own = lax.fori_loop(
        0, per_section, whole_frame, jnp.zeros((per_section, 3, count), jnp.float32)
    )
    members = lax.axis_size("member")
    first_sum, square_sum = in_one((own, jnp.sum(own * own, 1)), "member")
    mean_force = first_sum / members
    spread = jnp.maximum(square_sum / members - jnp.sum(mean_force * mean_force, 1), 0.0)
    atom_dev = jnp.sqrt(spread)
    max_dev = of_everyone_2(jnp.max(atom_dev, -1), "atoms")
    return (atom_dev, max_dev, mean_force)


def solution(mesh):
    return jax.shard_map(
        shards,
        mesh=mesh,
        in_specs=(
            P(None, None, "atoms"),
            P(None, "atoms"),
            P(None, "atoms", None),
            P(None, "atoms", None),
            P("member", None, None),
            P("member", "section", None),
            P("member", "section", None, None),
            P("member", "section", None, None),
            P("member", "section", None),
        ),
        out_specs=(P("section", "atoms"), P("section"), P("section", None, "atoms")),
        check_vma=False,
    )
```

profile of v0, /device:TPU:4, one launch (start us, length us, event | category | flops | bytes accessed | tf_op | source)
XLA Modules:
  0.0 235.5 jit_solution(9641796236025449721)
XLA Ops:
  3.3 14.9 %all_gather.3 = bf16[1,4,65668]{2,0,1:T(2,128)(2,1)S(1)} all-gather(bf16[1,1,65668]{2,0,1:T(2,128)(2,1)S(1)} %pad_maximum_fusion), channel_id=1, replica_groups=mesh['member'=8,'section'=4,'atoms'=8] {'section'}, dimensions={1}, use_global_device_ids=true | all-gather | bytes 656680 | tf_op jit(solution)/shard_map/all_gather | solution.py:30
  18.8 9.5 %all-to-all-start.4 = ((f32[8,8,3,128]{3,1,2,0:T(8,128)}), f32[8,8,3,128]{3,1,2,0:T(8,128)S(1)}, u32[]{:S(2)}, u32[]{:S(2)}) async-start(f32[8,8,3,128]{3,1,2,0:T(8,128)} %broadcast_in_dim.145), calls=%async_computation.4 | async-start | bytes 196608 | tf_op jit(solution)/shard_map/all_to_all | solution.py:11
  28.3 2.4 %slice_reduce_fusion = bf16[4,49152]{1,0:T(4,128)(2,1)S(1)} fusion(bf16[1,4,65668]{2,0,1:T(2,128)(2,1)S(1)} %all_gather.3), kind=kLoop, calls=%fused_computation.118 | loop fusion | bytes 786432 | tf_op jit(solution)/shard_map/split | solution.py:31
  31.7 7.1 %all-to-all-done.4 = f32[8,8,3,128]{3,1,2,0:T(8,128)S(1)} async-done(((f32[8,8,3,128]{3,1,2,0:T(8,128)}), f32[8,8,3,128]{3,1,2,0:T(8,128)S(1)}, u32[]{:S(2)}, u32[]{:S(2)}) %all-to-all-start.4) | async-done | bytes 98336 | tf_op jit(solution)/shard_map/all_to_all | solution.py:11
  38.9 170.6 %while.13 = (s32[]{:T(128)}, f32[2,3,128]{2,1,0:T(4,128)S(1)}, s32[]{:T(128)}, f32[8,3,1024]{2,1,0:T(4,128)S(1)}, f32[8,3,128]{2,0,1:T(8,128)S(1)}, /*index=5*/s...) while((s32[]{:T(128)}, f32[2,3,128]{2,1,0:T(4,128)S(1)}, ...), condition=%wide.region_7.8_spmd, body=%wide.region_0.7_spmd.sunk | while | flops 610847232 | bytes 40867676 | solution.py:144
  41.0 3.4 %all-to-all-start = ((bf16[8,128,128]{2,1,0:T(8,128)(2,1)}), bf16[8,128,128]{2,1,0:T(8,128)(2,1)S(1)}, u32[]{:S(2)}, u32[]{:S(2)}) async-start(bf16[8,128,128]{2,1,0:T(8,128)(2,1)} %broadcast_in_dim.152), calls=%async_computation | async-start | bytes 524288 | tf_op jit(solution)/shard_map/while/body/eval_jaxpr/all_to_all | solution.py:11
  45.8 12.3 %select_reduce_fusion.2 = f32[128,1024]{1,0:T(8,128)S(1)} fusion(f32[128,128]{1,0:T(8,128)S(1)} %get-tuple-element.459, s32[128,128]{1,0:T(8,128)S(1)} %get-tuple-element.460), kind=kLoop, calls=%fused_computation.clone.1 | loop fusion | flops 50200576 | bytes 655360 | tf_op jit(solution)/shard_map/while/body/eval_jaxpr/reduce_sum | solution.py:58
  62.3 9.5 %all-to-all-start.1 = ((bf16[8,128,128]{2,1,0:T(8,128)(2,1)}), bf16[8,128,128]{2,1,0:T(8,128)(2,1)S(1)}, u32[]{:S(2)}, u32[]{:S(2)}) async-start(bf16[8,128,128]{2,1,0:T(8,128)(2,1)} %broadcast_in_dim.153), calls=%async_computation.1 | async-start | bytes 524288 | tf_op jit(solution)/shard_map/while/body/eval_jaxpr/all_to_all | solution.py:11
  71.8 1.3 fusion.223
  73.4 10.0 %all-to-all-done.1 = bf16[8,128,128]{2,1,0:T(8,128)(2,1)S(1)} async-done(((bf16[8,128,128]{2,1,0:T(8,128)(2,1)}), bf16[8,128,128]{2,1,0:T(8,128)(2,1)S(1)}, u32[]{:S(2)}, u32[]{:S(2)}) %all-to-all-start.1) | async-done | bytes 262176 | tf_op jit(solution)/shard_map/while/body/eval_jaxpr/all_to_all | solution.py:11
  87.3 3.4 %all-to-all-start.2 = ((bf16[8,128,128]{2,1,0:T(8,128)(2,1)}), bf16[8,128,128]{2,1,0:T(8,128)(2,1)S(1)}, u32[]{:S(2)}, u32[]{:S(2)}) async-start(bf16[8,128,128]{2,1,0:T(8,128)(2,1)} %broadcast_in_dim.154), calls=%async_computation.2 | async-start | bytes 524288 | tf_op jit(solution)/shard_map/while/body/eval_jaxpr/all_to_all | solution.py:11
  90.7 1.3 fusion.221
  92.3 10.9 %all-to-all-done.2 = bf16[8,128,128]{2,1,0:T(8,128)(2,1)S(1)} async-done(((bf16[8,128,128]{2,1,0:T(8,128)(2,1)}), bf16[8,128,128]{2,1,0:T(8,128)(2,1)S(1)}, u32[]{:S(2)}, u32[]{:S(2)}) %all-to-all-start.2) | async-done | bytes 262176 | tf_op jit(solution)/shard_map/while/body/eval_jaxpr/all_to_all | solution.py:11
  107.0 3.4 %all-to-all-start.3 = ((bf16[8,128,128]{2,1,0:T(8,128)(2,1)}), bf16[8,128,128]{2,1,0:T(8,128)(2,1)S(1)}, u32[]{:S(2)}, u32[]{:S(2)}) async-start(bf16[8,128,128]{2,1,0:T(8,128)(2,1)} %broadcast_in_dim.155), calls=%async_computation.3 | async-start | bytes 524288 | tf_op jit(solution)/shard_map/while/body/eval_jaxpr/all_to_all | solution.py:11
  110.5 1.3 fusion.219
  112.0 9.7 %all-to-all-done.3 = bf16[8,128,128]{2,1,0:T(8,128)(2,1)S(1)} async-done(((bf16[8,128,128]{2,1,0:T(8,128)(2,1)}), bf16[8,128,128]{2,1,0:T(8,128)(2,1)S(1)}, u32[]{:S(2)}, u32[]{:S(2)}) %all-to-all-start.3) | async-done | bytes 262176 | tf_op jit(solution)/shard_map/while/body/eval_jaxpr/all_to_all | solution.py:11
  123.8 1.3 fusion.217
  127.1 3.4 %all-to-all-start = ((bf16[8,128,128]{2,1,0:T(8,128)(2,1)}), bf16[8,128,128]{2,1,0:T(8,128)(2,1)S(1)}, u32[]{:S(2)}, u32[]{:S(2)}) async-start(bf16[8,128,128]{2,1,0:T(8,128)(2,1)} %broadcast_in_dim.152), calls=%async_computation | async-start | bytes 524288 | tf_op jit(solution)/shard_map/while/body/eval_jaxpr/all_to_all | solution.py:11
  131.9 12.3 %select_reduce_fusion.2 = f32[128,1024]{1,0:T(8,128)S(1)} fusion(f32[128,128]{1,0:T(8,128)S(1)} %get-tuple-element.459, s32[128,128]{1,0:T(8,128)S(1)} %get-tuple-element.460), kind=kLoop, calls=%fused_computation.clone.1 | loop fusion | flops 50200576 | bytes 655360 | tf_op jit(solution)/shard_map/while/body/eval_jaxpr/reduce_sum | solution.py:58
  148.4 9.5 %all-to-all-start.1 = ((bf16[8,128,128]{2,1,0:T(8,128)(2,1)}), bf16[8,128,128]{2,1,0:T(8,128)(2,1)S(1)}, u32[]{:S(2)}, u32[]{:S(2)}) async-start(bf16[8,128,128]{2,1,0:T(8,128)(2,1)} %broadcast_in_dim.153), calls=%async_computation.1 | async-start | bytes 524288 | tf_op jit(solution)/shard_map/while/body/eval_jaxpr/all_to_all | solution.py:11
  157.9 1.3 fusion.223
  159.5 9.7 %all-to-all-done.1 = bf16[8,128,128]{2,1,0:T(8,128)(2,1)S(1)} async-done(((bf16[8,128,128]{2,1,0:T(8,128)(2,1)}), bf16[8,128,128]{2,1,0:T(8,128)(2,1)S(1)}, u32[]{:S(2)}, u32[]{:S(2)}) %all-to-all-start.1) | async-done | bytes 262176 | tf_op jit(solution)/shard_map/while/body/eval_jaxpr/all_to_all | solution.py:11
  173.0 3.4 %all-to-all-start.2 = ((bf16[8,128,128]{2,1,0:T(8,128)(2,1)}), bf16[8,128,128]{2,1,0:T(8,128)(2,1)S(1)}, u32[]{:S(2)}, u32[]{:S(2)}) async-start(bf16[8,128,128]{2,1,0:T(8,128)(2,1)} %broadcast_in_dim.154), calls=%async_computation.2 | async-start | bytes 524288 | tf_op jit(solution)/shard_map/while/body/eval_jaxpr/all_to_all | solution.py:11
  176.5 1.3 fusion.221
  178.1 9.6 %all-to-all-done.2 = bf16[8,128,128]{2,1,0:T(8,128)(2,1)S(1)} async-done(((bf16[8,128,128]{2,1,0:T(8,128)(2,1)}), bf16[8,128,128]{2,1,0:T(8,128)(2,1)S(1)}, u32[]{:S(2)}, u32[]{:S(2)}) %all-to-all-start.2) | async-done | bytes 262176 | tf_op jit(solution)/shard_map/while/body/eval_jaxpr/all_to_all | solution.py:11
  191.4 3.4 %all-to-all-start.3 = ((bf16[8,128,128]{2,1,0:T(8,128)(2,1)}), bf16[8,128,128]{2,1,0:T(8,128)(2,1)S(1)}, u32[]{:S(2)}, u32[]{:S(2)}) async-start(bf16[8,128,128]{2,1,0:T(8,128)(2,1)} %broadcast_in_dim.155), calls=%async_computation.3 | async-start | bytes 524288 | tf_op jit(solution)/shard_map/while/body/eval_jaxpr/all_to_all | solution.py:11
  194.9 1.3 fusion.219
  196.4 9.6 %all-to-all-done.3 = bf16[8,128,128]{2,1,0:T(8,128)(2,1)S(1)} async-done(((bf16[8,128,128]{2,1,0:T(8,128)(2,1)}), bf16[8,128,128]{2,1,0:T(8,128)(2,1)S(1)}, u32[]{:S(2)}, u32[]{:S(2)}) %all-to-all-start.3) | async-done | bytes 262176 | tf_op jit(solution)/shard_map/while/body/eval_jaxpr/all_to_all | solution.py:11
  208.1 1.3 fusion.217
  209.6 10.7 %all_to_all.57 = f32[8,1,1024]{2,1,0:T(1,128)S(1)} all-to-all(f32[8,1,1024]{2,1,0:T(1,128)S(1)} %broadcast_in_dim.146), channel_id=1, replica_groups=mesh['member'=8,'section'=4,'atoms'=8] {'member'}, dimensions={0} | all-to-all | bytes 65536 | tf_op jit(solution)/shard_map/all_to_all | solution.py:11
  221.6 3.3 %all-to-all-start.6 = ((f32[8,1,2]{2,1,0:T(1,128)}), f32[8,1,2]{2,1,0:T(1,128)S(1)}, u32[]{:S(2)}, u32[]{:S(2)}) async-start(f32[8,1,2]{2,1,0:T(1,128)} %broadcast_in_dim.147), calls=%async_computation.6 | async-start | bytes 8192 | tf_op jit(solution)/shard_map/all_to_all | solution.py:11
  225.5 9.4 %all-to-all-done.6 = f32[8,1,2]{2,1,0:T(1,128)S(1)} async-done(((f32[8,1,2]{2,1,0:T(1,128)}), f32[8,1,2]{2,1,0:T(1,128)S(1)}, u32[]{:S(2)}, u32[]{:S(2)}) %all-to-all-start.6) | async-done | bytes 96 | tf_op jit(solution)/shard_map/all_to_all | solution.py:11
  (156 shorter events, 42.6 us)
Async XLA Ops:
  1.4 16.8 %copy-start.1 = (f32[8,3,128]{2,0,1:T(8,128)S(1)}, f32[8,3,128]{2,0,1:T(8,128)}, u32[]{:S(2)}) copy-start(f32[8,3,128]{2,0,1:T(8,128)} %param.11) | copy-start | bytes 36868
  18.8 20.0 %all-to-all-start.4 = ((f32[8,8,3,128]{3,1,2,0:T(8,128)}), f32[8,8,3,128]{3,1,2,0:T(8,128)S(1)}, u32[]{:S(2)}, u32[]{:S(2)}) async-start(f32[8,8,3,128]{3,1,2,0:T(8,128)} %broadcast_in_dim.145), calls=%async_computation.4 | async-start | bytes 196608 | tf_op jit(solution)/shard_map/all_to_all | solution.py:11
  30.7 8.1 %copy-start = (bf16[1,128,128]{2,1,0:T(8,128)(2,1)S(1)}, bf16[1,128,128]{2,1,0:T(8,128)(2,1)}, u32[]{:S(2)}) copy-start(bf16[1,128,128]{2,1,0:T(8,128)(2,1)} %param.15) | copy-start | bytes 98308
  41.0 17.5 %all-to-all-start = ((bf16[8,128,128]{2,1,0:T(8,128)(2,1)}), bf16[8,128,128]{2,1,0:T(8,128)(2,1)S(1)}, u32[]{:S(2)}, u32[]{:S(2)}) async-start(bf16[8,128,128]{2,1,0:T(8,128)(2,1)} %broadcast_in_dim.152), calls=%async_computation | async-start | bytes 524288 | tf_op jit(solution)/shard_map/while/body/eval_jaxpr/all_to_all | solution.py:11
  62.3 21.2 %all-to-all-start.1 = ((bf16[8,128,128]{2,1,0:T(8,128)(2,1)}), bf16[8,128,128]{2,1,0:T(8,128)(2,1)S(1)}, u32[]{:S(2)}, u32[]{:S(2)}) async-start(bf16[8,128,128]{2,1,0:T(8,128)(2,1)} %broadcast_in_dim.153), calls=%async_computation.1 | async-start | bytes 524288 | tf_op jit(solution)/shard_map/while/body/eval_jaxpr/all_to_all | solution.py:11
  87.3 15.9 %all-to-all-start.2 = ((bf16[8,128,128]{2,1,0:T(8,128)(2,1)}), bf16[8,128,128]{2,1,0:T(8,128)(2,1)S(1)}, u32[]{:S(2)}, u32[]{:S(2)}) async-start(bf16[8,128,128]{2,1,0:T(8,128)(2,1)} %broadcast_in_dim.154), calls=%async_computation.2 | async-start | bytes 524288 | tf_op jit(solution)/shard_map/while/body/eval_jaxpr/all_to_all | solution.py:11
  107.0 14.6 %all-to-all-start.3 = ((bf16[8,128,128]{2,1,0:T(8,128)(2,1)}), bf16[8,128,128]{2,1,0:T(8,128)(2,1)S(1)}, u32[]{:S(2)}, u32[]{:S(2)}) async-start(bf16[8,128,128]{2,1,0:T(8,128)(2,1)} %broadcast_in_dim.155), calls=%async_computation.3 | async-start | bytes 524288 | tf_op jit(solution)/shard_map/while/body/eval_jaxpr/all_to_all | solution.py:11
  127.1 17.5 %all-to-all-start = ((bf16[8,128,128]{2,1,0:T(8,128)(2,1)}), bf16[8,128,128]{2,1,0:T(8,128)(2,1)S(1)}, u32[]{:S(2)}, u32[]{:S(2)}) async-start(bf16[8,128,128]{2,1,0:T(8,128)(2,1)} %broadcast_in_dim.152), calls=%async_computation | async-start | bytes 524288 | tf_op jit(solution)/shard_map/while/body/eval_jaxpr/all_to_all | solution.py:11
  148.4 20.8 %all-to-all-start.1 = ((bf16[8,128,128]{2,1,0:T(8,128)(2,1)}), bf16[8,128,128]{2,1,0:T(8,128)(2,1)S(1)}, u32[]{:S(2)}, u32[]{:S(2)}) async-start(bf16[8,128,128]{2,1,0:T(8,128)(2,1)} %broadcast_in_dim.153), calls=%async_computation.1 | async-start | bytes 524288 | tf_op jit(solution)/shard_map/while/body/eval_jaxpr/all_to_all | solution.py:11
  173.0 14.6 %all-to-all-start.2 = ((bf16[8,128,128]{2,1,0:T(8,128)(2,1)}), bf16[8,128,128]{2,1,0:T(8,128)(2,1)S(1)}, u32[]{:S(2)}, u32[]{:S(2)}) async-start(bf16[8,128,128]{2,1,0:T(8,128)(2,1)} %broadcast_in_dim.154), calls=%async_computation.2 | async-start | bytes 524288 | tf_op jit(solution)/shard_map/while/body/eval_jaxpr/all_to_all | solution.py:11
  191.4 14.5 %all-to-all-start.3 = ((bf16[8,128,128]{2,1,0:T(8,128)(2,1)}), bf16[8,128,128]{2,1,0:T(8,128)(2,1)S(1)}, u32[]{:S(2)}, u32[]{:S(2)}) async-start(bf16[8,128,128]{2,1,0:T(8,128)(2,1)} %broadcast_in_dim.155), calls=%async_computation.3 | async-start | bytes 524288 | tf_op jit(solution)/shard_map/while/body/eval_jaxpr/all_to_all | solution.py:11
  221.6 13.3 %all-to-all-start.6 = ((f32[8,1,2]{2,1,0:T(1,128)}), f32[8,1,2]{2,1,0:T(1,128)S(1)}, u32[]{:S(2)}, u32[]{:S(2)}) async-start(f32[8,1,2]{2,1,0:T(1,128)} %broadcast_in_dim.147), calls=%async_computation.6 | async-start | bytes 8192 | tf_op jit(solution)/shard_map/all_to_all | solution.py:11
where the time goes:
time: 238 us; the launch traced here: 235 us
  waiting for transfers between devices  76 us (32%)
  starting transfers between devices  52.4 us (22%)
  matrix products  32.6 us (14%)
  other arithmetic  30.5 us (13%)
  blocking collectives  25.6 us (11%)
  local copies, waits for them, and re-layouts  16.7 us (7%)
    all_to_all x10, waiting for transfers between devices, sent_to_all(): lax.all_to_all(jnp.broadcast_to(x[None], (devices, *x.shape)), axis, 0, 0...  76 us
    all_to_all x10, starting transfers between devices, sent_to_all(): lax.all_to_all(jnp.broadcast_to(x[None], (devices, *x.shape)), axis, 0, 0...  52.4 us
    reduce_sum x2, other arithmetic, geometry(): counts = jnp.sum(hit * mask.astype(jnp.float32)[:, :, None], 1)  24.7 us
    all_gather x1, blocking collectives, side_by_side(): whole = lax.all_gather(both, axis, axis=dim, tiled=True)  14.9 us
    all_to_all x1, blocking collectives, sent_to_all(): lax.all_to_all(jnp.broadcast_to(x[None], (devices, *x.shape)), axis, 0, 0...  10.7 us
    dot_general x8, matrix products, block_dev(): force = jnp.einsum('aj,caj->ca', pair_coef, delta) / slots  10.2 us
    dot_general x8, matrix products, block_dev(): pair_coef = jnp.einsum('h,haj->aj', coef.astype(jnp.float32), weights)  7.21 us
    broadcast_in_dim x11, local copies, waits for them, and re-layouts, sent_to_all(): jnp.broadcast_to(x[None], (devices, *x.shape))  7.15 us
  transfers between devices with their start and end apart: 10, of which 8 were waited for; matrix products, arithmetic and copies ran while one was open for 18% of the time, Pallas kernels for 0%

commit v1 on v0

v1 whole, which is shorter than its diff:
```python
import functools
import math

import jax
import jax.numpy as jnp
from jax import lax
from jax.experimental import pallas as pl
from jax.experimental.pallas import tpu as pltpu
from jax.sharding import PartitionSpec as P

F32 = jnp.float32
BF16 = jnp.bfloat16
NT = (((1,), (1,)), ((), ()))


def kernel(
    dims,
    pos_hbm,
    types_hbm,
    nbr_hbm,
    mask_hbm,
    table_hbm,
    gain_hbm,
    proj_hbm,
    outw_hbm,
    coef_hbm,
    dev_out,
    max_out,
    mean_out,
    pos_in,
    types_in,
    nbr_in,
    mask_in,
    table,
    gain_in,
    coef_in,
    pack_src,
    packs,
    code_own,
    code_src,
    code_got,
    gc_src,
    gcs,
    projs,
    outs,
    counts,
    half_pair,
    coef_sum,
    xs,
    x_first,
    kv,
    qm,
    acc,
    hs,
    f_src,
    f_all,
    d_src,
    d_all,
    in_sem,
    own_sem,
    pack_ss,
    pack_rs,
    code_ss,
    code_rs,
    w_ss,
    w_rs,
    x_ss,
    x_rs,
    f_ss,
    f_rs,
    d_ss,
    d_rs,
):
    n_member, n_section, n_y, heads, head_dim, slots = dims
    width = heads * head_dim
    n_atoms = 2 * n_y
    blk = 128
    rows = 2 * blk
    me = lax.axis_index("member")
    sec = lax.axis_index("section")
    at = lax.axis_index("atoms")
    y = at // 2
    zh = at % 2
    other = 1 - zh
    at_other = 2 * y + other

    frames2 = pl.ds(2 * sec, 2)
    loads = [
        pltpu.make_async_copy(nbr_hbm.at[frames2], nbr_in, in_sem.at[0]),
        pltpu.make_async_copy(mask_hbm.at[frames2], mask_in, in_sem.at[1]),
        pltpu.make_async_copy(pos_hbm.at[frames2], pos_in, in_sem.at[2]),
        pltpu.make_async_copy(types_hbm, types_in, in_sem.at[3]),
        pltpu.make_async_copy(gain_hbm, gain_in, in_sem.at[4]),
        pltpu.make_async_copy(coef_hbm, coef_in, in_sem.at[5]),
        pltpu.make_async_copy(table_hbm, table, in_sem.at[6]),
    ]
    own_w = [
        pltpu.make_async_copy(proj_hbm.at[0, 0], projs.at[sec], own_sem.at[0]),
        pltpu.make_async_copy(outw_hbm.at[0, 0], outs.at[sec], own_sem.at[1]),
    ]
    for c in loads + own_w:
        c.start()

    atom_peers = []
    for k in range(n_y):
        y2 = (y + k) % n_y
        if k:
            atom_peers.append((2 * y2 + zh, zh))
        atom_peers.append((2 * y2 + other, other))
    ring = [k for k in (1, n_y - 1, 2) if k < n_y]
    ring = list(dict.fromkeys(ring))
    sec_peers = [(sec + k) % n_section for k in dict.fromkeys((1, n_section - 1, 2))]
    same_side = [(me + k) % n_member for k in range(1, n_member)]
    far_side = [(me + k) % n_member for k in range(n_member)]

    barrier = pltpu.get_barrier_semaphore()
    n_partners = 0

    def greet(device):
        pl.semaphore_signal(barrier, inc=1, device_id=device, device_id_type=pl.DeviceIdType.MESH)

    for a2, _ in atom_peers[1:]:
        greet({"atoms": a2})
        n_partners += 1
    for s2 in sec_peers:
        greet({"section": s2})
        n_partners += 1
    for m2 in same_side:
        greet({"member": m2})
        n_partners += 1
    for m2 in far_side:
        greet({"member": m2, "atoms": at_other})
        n_partners += 1
    pl.semaphore_wait(barrier, n_partners)

    def remote(src, dst, ss, rs, device):
        return pltpu.make_async_remote_copy(
            src_ref=src,
            dst_ref=dst,
            send_sem=ss,
            recv_sem=rs,
            device_id=device,
            device_id_type=pl.DeviceIdType.MESH,
        )

    sent = []

    def send(*what):
        copy = remote(*what)
        copy.start()
        sent.append(copy)

    def got(dst, rs):
        remote(dst, dst, x_ss.at[0, 0, 0], rs, {"section": sec_peers[0]}).wait_recv()

    loads[0].wait()
    loads[1].wait()
    unused = rows * n_y
    code_src[...] = nbr_in[other] + jnp.where(mask_in[other] != 0, 0, unused)
    z_lo = me // 2
    mirror = (n_member // 2 - 1 - z_lo) * 2 + me % 2
    send(code_src, code_got, code_ss, code_rs, {"member": mirror, "atoms": at_other})

    loads[2].wait()
    loads[3].wait()
    pack_src[...] = jnp.zeros_like(pack_src)
    for z in range(2):
        pack_src[z, 0:3, :] = pos_in[z]
        pack_src[z, 3:4, :] = types_in[pl.ds(2 * sec + z, 1), :].astype(F32)
    packs[at] = pack_src[zh]
    for n, (a2, z2) in enumerate(atom_peers):
        send(pack_src.at[z2], packs.at[at], pack_ss.at[n], pack_rs.at[at], {"atoms": a2})

    loads[4].wait()
    loads[5].wait()
    gc_src[...] = jnp.zeros_like(gc_src)
    gc_src[0:1, :] = gain_in[0].astype(F32)
    gc_src[1:2, 0:heads] = coef_in[0].astype(F32)
    gcs[sec] = gc_src[...]
    for n, s2 in enumerate(sec_peers):
        to = {"section": s2}
        send(gc_src, gcs.at[sec], w_ss.at[0, n], w_rs.at[0, sec], to)
        send(proj_hbm.at[0, 0], projs.at[sec], w_ss.at[1, n], w_rs.at[1, sec], to)
        send(outw_hbm.at[0, 0], outs.at[sec], w_ss.at[2, n], w_rs.at[2, sec], to)

    code_own[...] = nbr_in[zh] + jnp.where(mask_in[zh] != 0, 0, unused)

    iota_hi = lax.broadcasted_iota(jnp.int32, (8, blk), 0)
    iota_lo = lax.broadcasted_iota(jnp.int32, (blk, blk), 0)
    none = jnp.zeros((8, blk), F32)

    def count(code_ref, first_row):
        def group(g, carry):
            code = code_ref[pl.ds(pl.multiple_of(g * 8, 8), 8), :]
            hi = lax.shift_right_logical(code, 7)
            lo = jnp.bitwise_and(code, blk - 1)
            for r in range(0, 8, 2):
                left = [jnp.where(iota_hi == hi[r + e : r + e + 1, :], 1.0, 0.0).astype(F32) for e in (0, 1)]
                lhs = jnp.concatenate(
                    [
                        jnp.concatenate([left[0], none], axis=1),
                        jnp.concatenate([none, left[1]], axis=1),
                    ],
                    axis=0,
                ).astype(BF16)
                rhs = jnp.concatenate(
                    [
                        jnp.where(iota_lo == lo[r + e : r + e + 1, :], 1.0, 0.0).astype(BF16)
                        for e in (0, 1)
                    ],
                    axis=1,
                )
                both = lax.dot_general(lhs, rhs, NT, preferred_element_type=F32)
                counts[pl.ds(pl.multiple_of((first_row + g * 8 + r) * 8, 8), 16), :] = both
            return carry

        lax.fori_loop(0, blk // 8, group, 0)

    count(code_own, zh * blk)

    for a2, _ in atom_peers:
        got(packs.at[a2], pack_rs.at[a2])
    got(code_got, code_rs)
    count(code_got, other * blk)

    own_cols = [jnp.transpose(packs[2 * y + r]) for r in range(2)]

    def pair_half(kb, carry):
        pj = packs[kb]
        c = kb // 2
        lanes = pl.ds(pl.multiple_of((kb % 2) * blk, blk), blk)
        for r in range(2):
            dist = jnp.zeros((blk, blk), F32)
            for d in range(3):
                delta = pj[d : d + 1, :] - own_cols[r][:, d : d + 1]
                dist = dist + delta * delta
            cnt = counts[pl.ds(r * blk * 8 + kb, blk, stride=8), :]
            half_pair[c, r * blk : (r + 1) * blk, lanes] = 0.5 * cnt / (1.0 + 0.125 * dist)
        return carry

    lax.fori_loop(0, n_atoms, pair_half, 0)

    def normed(hf, gain):
        return (hf * lax.rsqrt(jnp.mean(hf * hf, -1, keepdims=True) + 1e-06) * gain).astype(BF16)

    lane_head = lax.broadcasted_iota(jnp.int32, (blk, width), 1) // head_dim

    def queries(x, layer, r):
        q = jnp.dot(x, projs[layer, :, 0:width], preferred_element_type=F32)
        for h in range(heads):
            qm[r, h * blk : (h + 1) * blk, :] = jnp.where(lane_head == h, q, 0.0).astype(BF16)

    def weights_ready(layer):
        @pl.when(sec != layer)
        def _():
            got(gcs.at[layer], w_rs.at[0, layer])
            got(projs.at[layer], w_rs.at[1, layer])
            got(outs.at[layer], w_rs.at[2, layer])

    for c in own_w:
        c.wait()
    loads[6].wait()
    weights_ready(0)

    x_table = normed(table[0].astype(F32), gcs[0, 0:1, :])
    iota_type = lax.broadcasted_iota(jnp.int32, (blk, blk), 1).astype(F32)

    def first_rows(kb, carry):
        types = jnp.transpose(packs[kb])[:, 3:4]
        onehot = jnp.where(iota_type == types, 1.0, 0.0).astype(BF16)
        x = jnp.dot(onehot, x_table, preferred_element_type=F32).astype(BF16)
        x_first[kb // 2, pl.ds(pl.multiple_of((kb % 2) * blk, blk), blk), :] = x
        return carry

    lax.fori_loop(0, n_atoms, first_rows, 0)
    for r in range(2):
        onehot = jnp.where(iota_type == own_cols[r][:, 3:4], 1.0, 0.0).astype(BF16)
        hs[r] = jnp.dot(onehot, table[0], preferred_element_type=F32).astype(BF16)
        queries(x_first[y, r * blk : (r + 1) * blk, :], 0, r)

    to_tanh = 0.5 / math.sqrt(head_dim)

    def unit(layer, r, c):
        last = layer == n_section - 1
        here = slice(r * blk, (r + 1) * blk)
        s = lax.dot_general(qm[r], kv[c, :, 0:width], NT, preferred_element_type=F32)
        half = half_pair[c, here, :]
        total = None
        gated = []
        for h in range(heads):
            t = jnp.tanh(s[h * blk : (h + 1) * blk, :] * to_tanh)
            term = gcs[layer, 1:2, h : h + 1] * t
            total = term if total is None else total + term
            if not last:
                gated.append((half * t + half).astype(BF16))
        if layer == 0:
            coef_sum[c, here, :] = total
        else:
            coef_sum[c, here, :] += total
        if not last:
            acc[r] += jnp.dot(
                jnp.concatenate(gated, axis=0), kv[c, :, width:], preferred_element_type=F32
            )

    def ring_chunk(j):
        return (y + j + (j // 2) * (1 - 2 * (j % 2))) % n_y

    for layer in range(n_section):
        last = layer == n_section - 1
        for r in range(2):
            if not last:
                acc[r] = jnp.zeros_like(acc[r])

            def step(j, carry):
                c = ring_chunk(j)
                if r == 0:
                    if layer == 0:
                        x = x_first[c]
                    else:

                        @pl.when(j > 0)
                        def _():
                            for e in range(2):
                                got(
                                    xs.at[layer - 1, c, e * blk : (e + 1) * blk],
                                    x_rs.at[layer - 1, e, c],
                                )

                        x = xs[layer - 1, c]
                    n_kv = width if last else 2 * width
                    kv[c, :, 0:n_kv] = jnp.dot(
                        x, projs[layer, :, width : width + n_kv], preferred_element_type=F32
                    ).astype(BF16)
                unit(layer, r, c)
                return carry

            lax.fori_loop(0, n_y, step, 0)
            if last:
                continue
            if r == 0:
                weights_ready(layer + 1)
            message = jnp.zeros((blk, width), F32)
            for h in range(heads):
                message = message + jnp.where(
                    lane_head == h, acc[r, h * blk : (h + 1) * blk, :], 0.0
                )
            message = (message * (1.0 / slots)).astype(BF16)
            h_new = (
                hs[r].astype(F32) + jnp.dot(message, outs[layer], preferred_element_type=F32)
            ).astype(BF16)
            hs[r] = h_new
            x = normed(h_new.astype(F32), gcs[layer + 1, 0:1, :])
            part = xs.at[layer, y, r * blk : (r + 1) * blk]
            part[...] = x
            for n, k in enumerate(ring):
                send(
                    part,
                    part,
                    x_ss.at[layer, r, n],
                    x_rs.at[layer, r, y],
                    {"atoms": 2 * ((y + k) % n_y) + zh},
                )
            queries(x, layer + 1, r)

    coef_all = jnp.zeros((1, 1), F32)
    for layer in range(n_section):
        coef_all = coef_all + jnp.sum(gcs[layer, 1:2, :], axis=1, keepdims=True)
    column = lax.broadcasted_iota(jnp.int32, (blk, 8), 1)
    for r in range(2):

        def force(kb, carry):
            pj = packs[kb]
            c = kb // 2
            lanes = pl.ds(pl.multiple_of((kb % 2) * blk, blk), blk)
            here = slice(r * blk, (r + 1) * blk)
            pull = half_pair[c, here, lanes] * (coef_sum[c, here, lanes] + coef_all)
            return tuple(
                carry[d] + pull * (pj[d : d + 1, :] - own_cols[r][:, d : d + 1]) for d in range(3)
            )

        parts = lax.fori_loop(0, n_atoms, force, (jnp.zeros((blk, blk), F32),) * 3)
        tile = jnp.zeros((blk, 8), F32)
        for d in range(3):
            tile = jnp.where(column == d, jnp.sum(parts[d], axis=1, keepdims=True), tile)
        f_src[r] = jnp.transpose(tile) * (1.0 / slots)

    slot = zh * n_member + me
    f_all[slot] = f_src[zh]
    for n, m2 in enumerate(same_side):
        send(f_src.at[zh], f_all.at[slot], f_ss.at[n], f_rs.at[slot], {"member": m2})
    for n, m2 in enumerate(far_side):
        send(
            f_src.at[other],
            f_all.at[slot],
            f_ss.at[n_member + n],
            f_rs.at[slot],
            {"member": m2, "atoms": at_other},
        )
    for m2 in same_side:
        got(f_all.at[zh * n_member + m2], f_rs.at[zh * n_member + m2])
    for m2 in far_side:
        got(f_all.at[other * n_member + m2], f_rs.at[other * n_member + m2])

    devs = []
    for z in range(2):
        total = f_all[z * n_member]
        for m in range(1, n_member):
            total = total + f_all[z * n_member + m]
        mean = total * (1.0 / n_member)
        mean_out[z] = mean[0:3, :]
        square = jnp.zeros((8, blk), F32)
        for m in range(n_member):
            centered = f_all[z * n_member + m] - mean
            square = square + centered * centered
        devs.append(jnp.sqrt(jnp.sum(square, axis=0, keepdims=True) * (1.0 / n_member)))
    row = lax.broadcasted_iota(jnp.int32, (8, blk), 0)
    dev = jnp.where(row == 0, devs[0], jnp.where(row == 1, devs[1], 0.0))
    dev_out[...] = dev[0:2, :]
    d_src[...] = dev
    d_all[at] = dev
    for n, (a2, _) in enumerate(atom_peers):
        send(d_src, d_all.at[at], d_ss.at[n], d_rs.at[at], {"atoms": a2})
    for a2, _ in atom_peers:
        got(d_all.at[a2], d_rs.at[a2])
    top = d_all[0]
    for a2 in range(1, n_atoms):
        top = jnp.maximum(top, d_all[a2])
    for z in range(2):
        max_out[z] = jnp.max(top[z : z + 1, :])

    for copy in sent:
        copy.wait_send()


def shards(
    positions,
    atom_types,
    neighbors,
    nbr_mask,
    type_table,
    norm_gain,
    proj_weight,
    out_weight,
    force_coef,
):
    n_section = lax.axis_size("section")
    n_member = lax.axis_size("member")
    n_atoms = lax.axis_size("atoms")
    n_y = n_atoms // 2
    heads = force_coef.shape[2]
    width = type_table.shape[2]
    blk = atom_types.shape[1]
    slots = neighbors.shape[2]
    frames = atom_types.shape[0]
    rows = 2 * blk
    dims = (n_member, n_section, n_y, heads, width // heads, slots)
    dma = pltpu.SemaphoreType.DMA
    vmem = pltpu.VMEM
    scratch = [
        vmem((2, 3, blk), F32),
        vmem((frames, blk), jnp.int32),
        vmem((2, blk, slots), jnp.int32),
        vmem((2, blk, slots), jnp.int32),
        vmem(type_table.shape, BF16),
        vmem(norm_gain.shape, BF16),
        vmem(force_coef.shape, BF16),
        vmem((2, 8, blk), F32),
        vmem((n_atoms, 8, blk), F32),
        vmem((blk, slots), jnp.int32),
        vmem((blk, slots), jnp.int32),
        vmem((blk, slots), jnp.int32),
        vmem((8, width), F32),
        vmem((n_section, 8, width), F32),
        vmem((n_section, width, 3 * width), BF16),
        vmem((n_section, width, width), BF16),
        vmem((rows * 8, blk), F32),
        vmem((n_y, rows, rows), F32),
        vmem((n_y, rows, rows), F32),
        vmem((n_section - 1, n_y, rows, width), BF16),
        vmem((n_y, rows, width), BF16),
        vmem((n_y, rows, 2 * width), BF16),
        vmem((2, heads * blk, width), BF16),
        vmem((2, heads * blk, width), F32),
        vmem((2, blk, width), BF16),
        vmem((2, 8, blk), F32),
        vmem((2 * n_member, 8, blk), F32),
        vmem((8, blk), F32),
        vmem((n_atoms, 8, blk), F32),
        dma((7,)),
        dma((2,)),
        dma((n_atoms,)),
        dma((n_atoms,)),
        dma,
        dma,
        dma((3, n_section)),
        dma((3, n_section)),
        dma((n_section - 1, 2, n_y)),
        dma((n_section - 1, 2, n_y)),
        dma((2 * n_member,)),
        dma((2 * n_member,)),
        dma((n_atoms,)),
        dma((n_atoms,)),
    ]
    own_frames = frames // n_section
    atom_dev, max_dev, mean_force = pl.pallas_call(
        functools.partial(kernel, dims),
        out_shape=(
            jax.ShapeDtypeStruct((own_frames, blk), F32),
            jax.ShapeDtypeStruct((own_frames,), F32),
            jax.ShapeDtypeStruct((own_frames, 3, blk), F32),
        ),
        in_specs=[pl.BlockSpec(memory_space=pl.ANY)] * 9,
        out_specs=(
            pl.BlockSpec(memory_space=pltpu.VMEM),
            pl.BlockSpec(memory_space=pltpu.SMEM),
            pl.BlockSpec(memory_space=pltpu.VMEM),
        ),
        scratch_shapes=scratch,
        compiler_params=pltpu.CompilerParams(
            collective_id=0, has_side_effects=True, vmem_limit_bytes=40 * 1024 * 1024
        ),
        name="committee",
    )(
        positions,
        atom_types,
        neighbors,
        nbr_mask,
        type_table,
        norm_gain,
        proj_weight,
        out_weight,
        force_coef,
    )
    return (atom_dev, max_dev, mean_force)


def solution(mesh):
    return jax.shard_map(
        shards,
        mesh=mesh,
        in_specs=(
            P(None, None, "atoms"),
            P(None, "atoms"),
            P(None, "atoms", None),
            P(None, "atoms", None),
            P("member", None, None),
            P("member", "section", None),
            P("member", "section", None, None),
            P("member", "section", None, None),
            P("member", "section", None),
        ),
        out_specs=(P("section", "atoms"), P("section"), P("section", None, "atoms")),
        check_vma=False,
    )
```

time: 238 us -> 71.9 us (0.30)
  waiting for transfers between devices: 76 us -> 0 us
  Pallas kernels: 0 us -> 63.5 us
  starting transfers between devices: 52.4 us -> 0 us
  matrix products: 32.6 us -> 0 us
  other arithmetic: 30.5 us -> 0 us
  blocking collectives: 25.6 us -> 0 us
  local copies, waits for them, and re-layouts: 16.7 us -> 6.88 us
    all_to_all x10 -> x0, waiting for transfers between devices: 76 us -> none  [sent_to_all(): lax.all_to_all(jnp.broadcast_to(x[None], (devices, *x.shape)), axis, 0, 0...]
    pallas_call x0 -> x1, Pallas kernels: none -> 63.5 us  [shards(): pl.pallas_call(functools.partial(kernel, dims), out_shape=(jax.ShapeDtype...]
    all_to_all x10 -> x0, starting transfers between devices: 52.4 us -> none  [sent_to_all(): lax.all_to_all(jnp.broadcast_to(x[None], (devices, *x.shape)), axis, 0, 0...]
    dot_general x54 -> x0, matrix products: 32.6 us -> none  [the longest x8 10.2 us: block_dev(): force = jnp.einsum('aj,caj->ca', pair_coef, delta) / slots]
    reduce_sum x7 -> x0, other arithmetic: 25.2 us -> none  [the longest x2 24.7 us: geometry(): counts = jnp.sum(hit * mask.astype(jnp.float32)[:, :, None], 1)]
    all_gather x1 -> x0, blocking collectives: 14.9 us -> none  [side_by_side(): whole = lax.all_gather(both, axis, axis=dim, tiled=True)]
    all_to_all x1 -> x0, blocking collectives: 10.7 us -> none  [sent_to_all(): lax.all_to_all(jnp.broadcast_to(x[None], (devices, *x.shape)), axis, 0, 0...]
    broadcast_in_dim x11 -> x0, local copies, waits for them, and re-layouts: 7.15 us -> none  [sent_to_all(): jnp.broadcast_to(x[None], (devices, *x.shape))]
  transfers between devices with their start and end apart: 10 -> 0, of which waited for: 8 -> 0; matrix products, arithmetic and copies ran while one was open for 18% -> 0% of each run, Pallas kernels for 0% -> 0%
where the time goes in v1:
time: 71.9 us; the launch traced here: 71 us
  Pallas kernels  63.5 us (88%)
  local copies, waits for them, and re-layouts  6.88 us (10%)
    pallas_call x1, Pallas kernels, shards(): pl.pallas_call(functools.partial(kernel, dims), out_shape=(jax.ShapeDtype...  63.5 us
    unnamed x19, local copies, waits for them, and re-layouts  6.3 us

profile of v1, /device:TPU:4, one launch (start us, length us, event | category | flops | bytes accessed | tf_op | source)
XLA Modules:
  0.0 71.0 jit_solution(5877537489446339864)
XLA Ops:
  0.6 0.0 copy-start.7
  0.6 0.0 copy-start.6
  0.7 0.0 copy-start.5
  0.7 0.7 %copy.12.pos_hbm = f32[8,3,128]{2,1,0:T(4,128)S(1)} copy(f32[8,3,128]{2,0,1:T(8,128)} %param.9) | data formatting | bytes 24576 | tf_op args[0]
  1.4 0.0 copy-done.7
  1.4 0.0 copy-done.6
  1.4 0.0 copy-done.5
  1.4 0.0 copy-start
  1.4 1.0 %copy-done = s32[8,128,128]{2,1,0:T(8,128)S(1)} copy-done((s32[8,128,128]{2,1,0:T(8,128)S(1)}, s32[8,128,128]{2,1,0:T(8,128)}, u32[]{:S(2)}) %copy-start) | copy-done | bytes 524312
  2.5 0.0 copy-start.1
  2.5 1.0 %copy-done.1 = s32[8,128,128]{2,1,0:T(8,128)S(1)} copy-done((s32[8,128,128]{2,1,0:T(8,128)S(1)}, s32[8,128,128]{2,1,0:T(8,128)}, u32[]{:S(2)}) %copy-start.1) | copy-done | bytes 524312
  3.5 0.0 copy-start.2
  3.5 0.9 %copy-done.2 = bf16[1,1,128,384]{3,2,1,0:T(8,128)(2,1)S(1)} copy-done((bf16[1,1,128,384]{3,2,1,0:T(8,128)(2,1)S(1)}, bf16[1,1,128,384]{3,2,1,0:T(8,128)(2,1)}, u32[]{:S(2)}) %copy-start.2) | copy-done | bytes 98328
  4.4 0.0 copy-start.3
  4.4 0.8 %copy-done.3 = bf16[1,128,128]{2,1,0:T(8,128)(2,1)S(1)} copy-done((bf16[1,128,128]{2,1,0:T(8,128)(2,1)S(1)}, bf16[1,128,128]{2,1,0:T(8,128)(2,1)}, u32[]{:S(2)}) %copy-start.3) | copy-done | bytes 32792
  5.1 0.0 copy-start.4
  5.1 0.8 %copy-done.4 = bf16[1,1,128,128]{3,2,1,0:T(8,128)(2,1)S(1)} copy-done((bf16[1,1,128,128]{3,2,1,0:T(8,128)(2,1)S(1)}, bf16[1,1,128,128]{3,2,1,0:T(8,128)(2,1)}, u32[]{:S(2)}) %copy-start.4) | copy-done | bytes 32792
  5.9 63.5 %committee.1 = (f32[2,128]{1,0:T(2,128)S(1)}, f32[2]{0:T(128)S(1)}, f32[2,3,128]{2,1,0:T(4,128)S(1)}) custom-call(f32[8,3,128]{2,1,0:T(4,128)S(1)} %copy.12.pos_hbm, s32[8,128]{1,0:T(8,128)S(1)} %copy-done.5, s32[8,128,128]{2,1,0:T(8,128)S(1)} %copy-done, s32[8,128,128]{2,1,0:T(8,128)S(1)} %copy-done.1, bf16[1,128,128]{2,1,0:T(8,128)(2,1)S(1)} %copy-done.3, ...), custom_call_target="tpu_custom_call" | custom-call | tf_op jit(solution)/shard_map/committee/pallas_call | solution.py:505
  69.4 0.6 copy.13
  70.0 0.6 copy.16
  70.5 0.5 copy.17
Async XLA Ops:
  0.6 0.8 %copy-start.7 = (bf16[1,1,4]{2,1,0:T(2,128)(2,1)S(1)}, bf16[1,1,4]{2,1,0:T(2,128)(2,1)}, u32[]{:S(2)}) copy-start(bf16[1,1,4]{2,1,0:T(2,128)(2,1)} %coef_hbm.1) | copy-start | bytes 28
  0.6 0.8 %copy-start.6 = (bf16[1,1,128]{2,1,0:T(2,128)(2,1)S(1)}, bf16[1,1,128]{2,1,0:T(2,128)(2,1)}, u32[]{:S(2)}) copy-start(bf16[1,1,128]{2,1,0:T(2,128)(2,1)} %gain_hbm.1) | copy-start | bytes 772
  0.7 0.8 %copy-start.5 = (s32[8,128]{1,0:T(8,128)S(1)}, s32[8,128]{1,0:T(8,128)}, u32[]{:S(2)}) copy-start(s32[8,128]{1,0:T(8,128)} %types_hbm.1) | copy-start | bytes 12292
  1.4 1.0 %copy-start = (s32[8,128,128]{2,1,0:T(8,128)S(1)}, s32[8,128,128]{2,1,0:T(8,128)}, u32[]{:S(2)}) copy-start(s32[8,128,128]{2,1,0:T(8,128)} %nbr_hbm.1) | copy-start | bytes 1572868
  2.5 1.0 %copy-start.1 = (s32[8,128,128]{2,1,0:T(8,128)S(1)}, s32[8,128,128]{2,1,0:T(8,128)}, u32[]{:S(2)}) copy-start(s32[8,128,128]{2,1,0:T(8,128)} %mask_hbm.1) | copy-start | bytes 1572868
  3.5 0.9 %copy-start.2 = (bf16[1,1,128,384]{3,2,1,0:T(8,128)(2,1)S(1)}, bf16[1,1,128,384]{3,2,1,0:T(8,128)(2,1)}, u32[]{:S(2)}) copy-start(bf16[1,1,128,384]{3,2,1,0:T(8,128)(2,1)} %proj_hbm.1) | copy-start | bytes 294916
  4.4 0.8 %copy-start.3 = (bf16[1,128,128]{2,1,0:T(8,128)(2,1)S(1)}, bf16[1,128,128]{2,1,0:T(8,128)(2,1)}, u32[]{:S(2)}) copy-start(bf16[1,128,128]{2,1,0:T(8,128)(2,1)} %table_hbm.1) | copy-start | bytes 98308
  5.1 0.8 %copy-start.4 = (bf16[1,1,128,128]{3,2,1,0:T(8,128)(2,1)S(1)}, bf16[1,1,128,128]{3,2,1,0:T(8,128)(2,1)}, u32[]{:S(2)}) copy-start(bf16[1,1,128,128]{3,2,1,0:T(8,128)(2,1)} %outw_hbm.1) | copy-start | bytes 98308

commit v2 on v1

v2 whole, which is shorter than its diff:
```python
import functools
import math

import jax
import jax.numpy as jnp
from jax import lax
from jax.experimental import pallas as pl
from jax.experimental.pallas import tpu as pltpu
from jax.sharding import PartitionSpec as P

F32 = jnp.float32
BF16 = jnp.bfloat16
NT = (((1,), (1,)), ((), ()))


def kernel(
    dims,
    pos_hbm,
    types_hbm,
    nbr_hbm,
    mask_hbm,
    table_hbm,
    gain_hbm,
    proj_hbm,
    outw_hbm,
    coef_hbm,
    result,
    pos_in,
    types_in,
    nbr_in,
    mask_in,
    table,
    gain_in,
    coef_in,
    pack_src,
    packs,
    code_own,
    code_src,
    code_got,
    gc_src,
    gcs,
    projs,
    outs,
    counts,
    half_pair,
    coef_sum,
    xs,
    kv,
    qm,
    acc,
    hs,
    f_all,
    d_all,
    in_sem,
    pack_ss,
    pack_rs,
    code_ss,
    code_rs,
    w_ss,
    w_rs,
    x_ss,
    x_rs,
    f_ss,
    f_rs,
    d_ss,
    d_rs,
):
    n_member, n_section, n_y, heads, head_dim, slots = dims
    width = heads * head_dim
    n_atoms = 2 * n_y
    blk = 128
    me = lax.axis_index("member")
    sec = lax.axis_index("section")
    at = lax.axis_index("atoms")
    y = at // 2
    zh = at % 2
    other = 1 - zh
    sides = (zh, other)
    mirror = (n_member // 2 - 1 - me // 2) * 2 + me % 2

    turns = list(dict.fromkeys(k for k in (1, n_y - 1, 2) if 0 < k < n_y))
    ring = [(y + k) % n_y for k in turns]
    near = [{"atoms": 2 * y2 + zh} for y2 in ring]
    across = [{"atoms": 2 * y2 + other, "member": mirror} for y2 in [y] + ring]
    sec_turns = list(dict.fromkeys((1, n_section - 1, 2)))
    sec_peers = [{"section": (sec + k) % n_section} for k in sec_turns]
    mates = [(me + k) % n_member for k in range(1, n_member)]

    barrier = pltpu.get_barrier_semaphore()
    partners = across + near + sec_peers + [{"member": m2} for m2 in mates]
    for device in partners:
        pl.semaphore_signal(barrier, inc=1, device_id=device, device_id_type=pl.DeviceIdType.MESH)

    frames2 = pl.ds(2 * sec, 2)
    loads = [
        pltpu.make_async_copy(nbr_hbm.at[frames2], nbr_in, in_sem.at[0]),
        pltpu.make_async_copy(mask_hbm.at[frames2], mask_in, in_sem.at[1]),
        pltpu.make_async_copy(pos_hbm, pos_in, in_sem.at[2]),
        pltpu.make_async_copy(types_hbm, types_in, in_sem.at[3]),
        pltpu.make_async_copy(gain_hbm, gain_in, in_sem.at[4]),
        pltpu.make_async_copy(coef_hbm, coef_in, in_sem.at[5]),
        pltpu.make_async_copy(proj_hbm.at[0, 0], projs.at[sec], in_sem.at[6]),
        pltpu.make_async_copy(outw_hbm.at[0, 0], outs.at[sec], in_sem.at[7]),
        pltpu.make_async_copy(table_hbm, table, in_sem.at[8]),
    ]
    for c in loads:
        c.start()

    def remote(src, dst, ss, rs, device):
        return pltpu.make_async_remote_copy(
            src_ref=src,
            dst_ref=dst,
            send_sem=ss,
            recv_sem=rs,
            device_id=device,
            device_id_type=pl.DeviceIdType.MESH,
        )

    sent = []

    def send(*what):
        copy = remote(*what)
        copy.start()
        sent.append(copy)

    def got(dst, rs):
        remote(dst, dst, x_ss.at[0, 0, 0], rs, sec_peers[0]).wait_recv()

    loads[0].wait()
    loads[1].wait()
    unused = n_atoms * blk
    code_src[...] = nbr_in[other] + jnp.where(mask_in[other] != 0, 0, unused)
    code_own[...] = nbr_in[zh] + jnp.where(mask_in[zh] != 0, 0, unused)

    loads[2].wait()
    loads[3].wait()
    pack_src[...] = jnp.zeros_like(pack_src)
    for r in range(2):
        frame = pl.ds(2 * sec + sides[r], 1)
        for d in range(3):
            pack_src[r, d : d + 1, :] = pos_in[d, frame, :]
        pack_src[r, 3:4, :] = types_in[frame, :].astype(F32)
    packs[at] = pack_src[0]
    loads[4].wait()
    loads[5].wait()
    gc_src[...] = jnp.zeros_like(gc_src)
    gc_src[0:1, :] = gain_in[0].astype(F32)
    gc_src[1:2, 0:heads] = coef_in[0].astype(F32)
    gcs[sec] = gc_src[...]

    pl.semaphore_wait(barrier, len(partners))
    send(code_src, code_got, code_ss, code_rs, across[0])
    for n, to in enumerate(near + across):
        r = 0 if n < len(near) else 1
        send(pack_src.at[r], packs.at[at], pack_ss.at[n], pack_rs.at[at], to)
    for n, to in enumerate(sec_peers):
        send(gc_src, gcs.at[sec], w_ss.at[0, n], w_rs.at[0, sec], to)
        send(proj_hbm.at[0, 0], projs.at[sec], w_ss.at[1, n], w_rs.at[1, sec], to)
        send(outw_hbm.at[0, 0], outs.at[sec], w_ss.at[2, n], w_rs.at[2, sec], to)

    iota_hi = lax.broadcasted_iota(jnp.int32, (8, blk), 0)
    iota_lo = lax.broadcasted_iota(jnp.int32, (blk, blk), 0)
    none = jnp.zeros((8, blk), F32)

    def count(code_ref, r):
        per = 16

        def group(g, carry):
            code = code_ref[pl.ds(pl.multiple_of(g * per, per), per), :]
            hi = lax.shift_right_logical(code, 7)
            lo = jnp.bitwise_and(code, blk - 1)
            for i in range(0, per, 2):
                left = [
                    jnp.where(iota_hi == hi[i + e : i + e + 1, :], 1.0, 0.0).astype(F32)
                    for e in (0, 1)
                ]
                lhs = jnp.concatenate(
                    [
                        jnp.concatenate([left[0], none], axis=1),
                        jnp.concatenate([none, left[1]], axis=1),
                    ],
                    axis=0,
                ).astype(BF16)
                rhs = jnp.concatenate(
                    [
                        jnp.where(iota_lo == lo[i + e : i + e + 1, :], 1.0, 0.0).astype(BF16)
                        for e in (0, 1)
                    ],
                    axis=1,
                )
                both = lax.dot_general(lhs, rhs, NT, preferred_element_type=F32)
                counts[pl.ds(pl.multiple_of((r * blk + g * per + i) * 8, 16), 16), :] = both
            return carry

        lax.fori_loop(0, blk // per, group, 0)

    count(code_own, 0)

    for y2 in ring:
        got(packs.at[2 * y2 + zh], pack_rs.at[2 * y2 + zh])
    for y2 in [y] + ring:
        got(packs.at[2 * y2 + other], pack_rs.at[2 * y2 + other])

    own_cols = [jnp.transpose(packs[2 * y + sides[r]]) for r in range(2)]

    def pair_half(r):
        for kb in range(n_atoms):
            pj = packs[kb]
            dist = jnp.zeros((blk, blk), F32)
            for d in range(3):
                delta = pj[d : d + 1, :] - own_cols[r][:, d : d + 1]
                dist = dist + delta * delta
            cnt = counts[pl.ds(r * blk * 8 + kb, blk, stride=8), :]
            half_pair[r, kb] = 0.5 * cnt / (1.0 + 0.125 * dist)

    pair_half(0)

    def normed(hf, gain):
        return (hf * lax.rsqrt(jnp.mean(hf * hf, -1, keepdims=True) + 1e-06) * gain).astype(BF16)

    lane_head = lax.broadcasted_iota(jnp.int32, (blk, width), 1) // head_dim

    def heads_apart(q, r):
        for h in range(heads):
            qm[r, h * blk : (h + 1) * blk, :] = jnp.where(lane_head == h, q, 0.0).astype(BF16)

    def queries(x, layer, r):
        heads_apart(jnp.dot(x, projs[layer, :, 0:width], preferred_element_type=F32), r)

    def keys(x, layer, kb):
        n_kv = width if layer == n_section - 1 else 2 * width
        kv[layer % 2, kb, :, 0:n_kv] = jnp.dot(
            x, projs[layer, :, width : width + n_kv], preferred_element_type=F32
        ).astype(BF16)

    def weights_ready(layer):
        @pl.when(sec != layer)
        def _():
            got(gcs.at[layer], w_rs.at[0, layer])
            got(projs.at[layer], w_rs.at[1, layer])
            got(outs.at[layer], w_rs.at[2, layer])

    for c in loads[6:]:
        c.wait()
    weights_ready(0)

    x_table = normed(table[0].astype(F32), gcs[0, 0:1, :])
    qkv_table = jnp.dot(x_table, projs[0], preferred_element_type=F32).astype(BF16)
    iota_type = lax.broadcasted_iota(jnp.int32, (blk, blk), 1).astype(F32)

    def onehot(columns):
        return jnp.where(iota_type == columns[:, 3:4], 1.0, 0.0).astype(BF16)

    for kb in range(n_atoms):
        kv[0, kb] = jnp.dot(
            onehot(jnp.transpose(packs[kb])), qkv_table[:, width:], preferred_element_type=F32
        ).astype(BF16)
    for r in range(2):
        which = onehot(own_cols[r])
        hs[r] = jnp.dot(which, table[0], preferred_element_type=F32).astype(BF16)
        heads_apart(jnp.dot(which, qkv_table[:, 0:width], preferred_element_type=F32), r)

    to_tanh = 0.5 / math.sqrt(head_dim)

    def unit(layer, r, blocks, first):
        last = layer == n_section - 1
        k = jnp.concatenate([kv[layer % 2, kb, :, 0:width] for kb in blocks], axis=0)
        s = lax.dot_general(qm[r], k, NT, preferred_element_type=F32)
        half = jnp.concatenate([half_pair[r, kb] for kb in blocks], axis=1)
        total = None
        gated = []
        for h in range(heads):
            t = jnp.tanh(s[h * blk : (h + 1) * blk, :] * to_tanh)
            term = gcs[layer, 1:2, h : h + 1] * t
            total = term if total is None else total + term
            if not last:
                gated.append((half * t + half).astype(BF16))
        for n, kb in enumerate(blocks):
            piece = total[:, n * blk : (n + 1) * blk]
            if layer == 0:
                coef_sum[r, kb] = piece
            else:
                coef_sum[r, kb] += piece
        if not last:
            v = jnp.concatenate([kv[layer % 2, kb, :, width:] for kb in blocks], axis=0)
            part = jnp.dot(jnp.concatenate(gated, axis=0), v, preferred_element_type=F32)
            if first:
                acc[r] = part
            else:
                acc[r] += part

    def finish(layer, r):
        message = acc[r, 0:blk, :]
        for h in range(1, heads):
            message = jnp.where(lane_head == h, acc[r, h * blk : (h + 1) * blk, :], message)
        message = (message * (1.0 / slots)).astype(BF16)
        h_new = (
            hs[r].astype(F32) + jnp.dot(message, outs[layer], preferred_element_type=F32)
        ).astype(BF16)
        hs[r] = h_new
        x = normed(h_new.astype(F32), gcs[layer + 1, 0:1, :])
        mine = 2 * y + sides[r]
        xs[layer, mine] = x
        part = xs.at[layer, mine]
        for n, to in enumerate(near):
            send(part, part, x_ss.at[layer, r, n], x_rs.at[layer, mine], to)
        queries(x, layer + 1, r)
        keys(x, layer + 1, mine)

    def arrived(layer, y2, r):
        kb = 2 * y2 + sides[r]
        got(xs.at[layer - 1, kb], x_rs.at[layer - 1, kb])
        keys(xs[layer - 1, kb], layer, kb)

    own_pair = (2 * y + zh, 2 * y + other)
    first_halves = [2 * y2 + zh for y2 in ring]
    second_halves = [2 * y2 + other for y2 in ring]
    rest = first_halves + second_halves
    groups = [own_pair] + [tuple(rest[i : i + 2]) for i in range(0, len(rest), 2)]

    for n, g in enumerate(groups):
        unit(0, 0, g, n == 0)
    weights_ready(1)
    finish(0, 0)
    got(code_got, code_rs)
    count(code_got, 1)
    pair_half(1)
    for n, g in enumerate(groups):
        unit(0, 1, g, n == 0)
    finish(0, 1)

    for layer in range(1, n_section):
        last = layer == n_section - 1
        for r in range(2):
            unit(layer, r, groups[0], True)
        for y2 in ring:
            arrived(layer, y2, 0)
        for r in range(2):
            unit(layer, r, groups[1], False)
        if not last:
            weights_ready(layer + 1)
        for y2 in ring:
            arrived(layer, y2, 1)
        for r in range(2):
            for g in groups[2:]:
                unit(layer, r, g, False)
            if not last:
                finish(layer, r)

    coef_all = jnp.zeros((1, 1), F32)
    for layer in range(n_section):
        coef_all = coef_all + jnp.sum(gcs[layer, 1:2, :], axis=1, keepdims=True)
    column = lax.broadcasted_iota(jnp.int32, (blk, 8), 1)
    tile = jnp.zeros((blk, 8), F32)
    for r in range(2):
        parts = [jnp.zeros((blk, blk), F32)] * 3
        for kb in range(n_atoms):
            pj = packs[kb]
            pull = half_pair[r, kb] * (coef_sum[r, kb] + coef_all)
            for d in range(3):
                parts[d] = parts[d] + pull * (pj[d : d + 1, :] - own_cols[r][:, d : d + 1])
        for d in range(3):
            tile = jnp.where(
                column == 4 * r + d, jnp.sum(parts[d], axis=1, keepdims=True), tile
            )
    f_all[me] = jnp.transpose(tile) * (1.0 / slots)
    for n, m2 in enumerate(mates):
        send(f_all.at[me], f_all.at[me], f_ss.at[n], f_rs.at[me], {"member": m2})
    for m2 in mates:
        got(f_all.at[m2], f_rs.at[m2])

    total = f_all[0]
    for m in range(1, n_member):
        total = total + f_all[m]
    mean = total * (1.0 / n_member)
    square = jnp.zeros((8, blk), F32)
    for m in range(n_member):
        centered = f_all[m] - mean
        square = square + centered * centered
    dev = [
        jnp.sqrt(jnp.sum(square[4 * r : 4 * r + 4], axis=0, keepdims=True) * (1.0 / n_member))
        for r in range(2)
    ]
    row = lax.broadcasted_iota(jnp.int32, (8, blk), 0)
    top = jnp.where(row == 4, jnp.maximum(dev[0], dev[1]), 0.0)
    mean_far = jnp.concatenate([mean[4:8], mean[0:4]], axis=0)
    d_all[at] = jnp.where(row < 3, mean_far, jnp.where(row == 3, dev[1], top))
    for n, to in enumerate(near + across):
        send(d_all.at[at], d_all.at[at], d_ss.at[n], d_rs.at[at], to)
    result[zh] = jnp.where(row < 3, mean, jnp.where(row == 3, dev[0], 0.0))
    for y2 in ring:
        got(d_all.at[2 * y2 + zh], d_rs.at[2 * y2 + zh])
    for y2 in [y] + ring:
        got(d_all.at[2 * y2 + other], d_rs.at[2 * y2 + other])
    result[other] = d_all[2 * y + other]
    for z in range(2):
        best = d_all[z]
        for y2 in range(1, n_y):
            best = jnp.maximum(best, d_all[2 * y2 + z])
        result[z, 4:5, :] = best[4:5, :]

    for copy in sent:
        copy.wait_send()


def finish_outputs(result, dev_out, max_out, mean_out):
    for z in range(2):
        for d in range(3):
            mean_out[d, z : z + 1, :] = result[z, d : d + 1, :]
        dev_out[z : z + 1, :] = result[z, 3:4, :]
        max_out[z] = jnp.max(result[z, 4:5, :])


def shards(
    positions,
    atom_types,
    neighbors,
    nbr_mask,
    type_table,
    norm_gain,
    proj_weight,
    out_weight,
    force_coef,
):
    n_section = lax.axis_size("section")
    n_member = lax.axis_size("member")
    n_atoms = lax.axis_size("atoms")
    n_y = n_atoms // 2
    heads = force_coef.shape[2]
    width = type_table.shape[2]
    blk = atom_types.shape[1]
    slots = neighbors.shape[2]
    frames = atom_types.shape[0]
    dims = (n_member, n_section, n_y, heads, width // heads, slots)
    dma = pltpu.SemaphoreType.DMA
    vmem = pltpu.VMEM
    scratch = [
        vmem((3, frames, blk), F32),
        vmem((frames, blk), jnp.int32),
        vmem((2, blk, slots), jnp.int32),
        vmem((2, blk, slots), jnp.int32),
        vmem(type_table.shape, BF16),
        vmem(norm_gain.shape, BF16),
        vmem(force_coef.shape, BF16),
        vmem((2, 8, blk), F32),
        vmem((n_atoms, 8, blk), F32),
        vmem((blk, slots), jnp.int32),
        vmem((blk, slots), jnp.int32),
        vmem((blk, slots), jnp.int32),
        vmem((8, width), F32),
        vmem((n_section, 8, width), F32),
        vmem((n_section, width, 3 * width), BF16),
        vmem((n_section, width, width), BF16),
        vmem((2 * blk * 8, blk), F32),
        vmem((2, n_atoms, blk, blk), F32),
        vmem((2, n_atoms, blk, blk), F32),
        vmem((n_section - 1, n_atoms, blk, width), BF16),
        vmem((2, n_atoms, blk, 2 * width), BF16),
        vmem((2, heads * blk, width), BF16),
        vmem((2, heads * blk, width), F32),
        vmem((2, blk, width), BF16),
        vmem((n_member, 8, blk), F32),
        vmem((n_atoms, 8, blk), F32),
        dma((9,)),
        dma((n_atoms,)),
        dma((n_atoms,)),
        dma,
        dma,
        dma((3, n_section)),
        dma((3, n_section)),
        dma((n_section - 1, 2, n_y)),
        dma((n_section - 1, n_atoms)),
        dma((n_member,)),
        dma((n_member,)),
        dma((n_atoms,)),
        dma((n_atoms,)),
    ]
    own_frames = frames // n_section
    result = pl.pallas_call(
        functools.partial(kernel, dims),
        out_shape=jax.ShapeDtypeStruct((own_frames, 8, blk), F32),
        in_specs=[pl.BlockSpec(memory_space=pltpu.HBM)] * 9,
        out_specs=pl.BlockSpec(memory_space=pltpu.VMEM),
        scratch_shapes=scratch,
        compiler_params=pltpu.CompilerParams(
            collective_id=0, has_side_effects=True, vmem_limit_bytes=56 * 1024 * 1024
        ),
        name="committee",
    )(
        jnp.transpose(positions, (1, 0, 2)),
        atom_types,
        neighbors,
        nbr_mask,
        type_table,
        norm_gain,
        proj_weight,
        out_weight,
        force_coef,
    )
    atom_dev, max_dev, mean_force = pl.pallas_call(
        finish_outputs,
        out_shape=(
            jax.ShapeDtypeStruct((own_frames, blk), F32),
            jax.ShapeDtypeStruct((own_frames,), F32),
            jax.ShapeDtypeStruct((3, own_frames, blk), F32),
        ),
        in_specs=[pl.BlockSpec(memory_space=pltpu.VMEM)],
        out_specs=(
            pl.BlockSpec(memory_space=pltpu.VMEM),
            pl.BlockSpec(memory_space=pltpu.SMEM),
            pl.BlockSpec(memory_space=pltpu.VMEM),
        ),
        name="outputs",
    )(result)
    return (atom_dev, max_dev, jnp.transpose(mean_force, (1, 0, 2)))


def solution(mesh):
    return jax.shard_map(
        shards,
        mesh=mesh,
        in_specs=(
            P(None, None, "atoms"),
            P(None, "atoms"),
            P(None, "atoms", None),
            P(None, "atoms", None),
            P("member", None, None),
            P("member", "section", None),
            P("member", "section", None, None),
            P("member", "section", None, None),
            P("member", "section", None),
        ),
        out_specs=(P("section", "atoms"), P("section"), P("section", None, "atoms")),
        check_vma=False,
    )
```

time: 71.9 us -> 51.3 us (0.71)
  the two profiles are of different devices: /device:TPU:4 before, /device:TPU:1 now
where the time goes in v2:
time: 51.3 us; the launch traced here: 51.2 us
  Pallas kernels  50.5 us (98%)
  between operations  0.64 us (1%)
    pallas_call x1, Pallas kernels, shards(): pl.pallas_call(functools.partial(kernel, dims), out_shape=jax.ShapeDtypeS...  49.2 us
    pallas_call x1, Pallas kernels, shards(): pl.pallas_call(finish_outputs, out_shape=(jax.ShapeDtypeStruct((own_frame...  1.34 us

profile of v2, /device:TPU:1, one launch (start us, length us, event | category | flops | bytes accessed | tf_op | source)
XLA Modules:
  0.0 51.2 jit_solution(10253172277904558052)
XLA Ops:
  0.6 49.2 %committee.1.result = f32[2,8,128]{2,1,0:T(8,128)} custom-call(f32[3,8,128]{2,1,0:T(8,128)} %bitcast.2, s32[8,128]{1,0:T(8,128)} %types_hbm.1, s32[8,128,128]{2,1,0:T(8,128)} %nbr_hbm.1, s32[8,128,128]{2,1,0:T(8,128)} %mask_hbm.1, bf16[1,128,128]{2,1,0:T(8,128)(2,1)} %table_hbm.1, bf16[1,1,128]{2,1,0:T(2,128)(2,1)} %gain_hbm.1, ...), custom_call_target="tpu_custom_call" | custom-call | tf_op jit(solution)/shard_map/committee/pallas_call | solution.py:479
  49.8 1.3 %outputs.1 = (f32[2,128]{1,0:T(2,128)}, f32[2]{0:T(128)}, f32[3,2,128]{2,1,0:T(2,128)}) custom-call(f32[2,8,128]{2,1,0:T(8,128)} %committee.1.result), custom_call_target="tpu_custom_call" | custom-call | tf_op jit(solution)/shard_map/outputs/pallas_call | solution.py:500

commit v3 on v2

--- a/solution.py
+++ b/solution.py
@@ -24,7 +24,9 @@
     proj_hbm,
     outw_hbm,
     coef_hbm,
-    result,
+    dev_out,
+    max_out,
+    mean_out,
     pos_in,
     types_in,
     nbr_in,
@@ -93,10 +95,10 @@
 
     frames2 = pl.ds(2 * sec, 2)
     loads = [
-        pltpu.make_async_copy(nbr_hbm.at[frames2], nbr_in, in_sem.at[0]),
-        pltpu.make_async_copy(mask_hbm.at[frames2], mask_in, in_sem.at[1]),
-        pltpu.make_async_copy(pos_hbm, pos_in, in_sem.at[2]),
-        pltpu.make_async_copy(types_hbm, types_in, in_sem.at[3]),
+        pltpu.make_async_copy(pos_hbm, pos_in, in_sem.at[0]),
+        pltpu.make_async_copy(types_hbm, types_in, in_sem.at[1]),
+        pltpu.make_async_copy(nbr_hbm.at[frames2], nbr_in, in_sem.at[2]),
+        pltpu.make_async_copy(mask_hbm.at[frames2], mask_in, in_sem.at[3]),
         pltpu.make_async_copy(gain_hbm, gain_in, in_sem.at[4]),
         pltpu.make_async_copy(coef_hbm, coef_in, in_sem.at[5]),
         pltpu.make_async_copy(proj_hbm.at[0, 0], projs.at[sec], in_sem.at[6]),
@@ -128,12 +130,6 @@
 
     loads[0].wait()
     loads[1].wait()
-    unused = n_atoms * blk
-    code_src[...] = nbr_in[other] + jnp.where(mask_in[other] != 0, 0, unused)
-    code_own[...] = nbr_in[zh] + jnp.where(mask_in[zh] != 0, 0, unused)
-
-    loads[2].wait()
-    loads[3].wait()
     pack_src[...] = jnp.zeros_like(pack_src)
     for r in range(2):
         frame = pl.ds(2 * sec + sides[r], 1)
@@ -141,80 +137,77 @@
             pack_src[r, d : d + 1, :] = pos_in[d, frame, :]
         pack_src[r, 3:4, :] = types_in[frame, :].astype(F32)
     packs[at] = pack_src[0]
+    pl.semaphore_wait(barrier, len(partners))
+    for n, to in enumerate(across):
+        send(pack_src.at[1], packs.at[at], pack_ss.at[n], pack_rs.at[at], to)
+
+    loads[2].wait()
+    loads[3].wait()
+    unused = n_atoms * blk
+    code_src[...] = nbr_in[other] + jnp.where(mask_in[other] != 0, 0, unused)
+    send(code_src, code_got, code_ss, code_rs, across[0])
+    for n, to in enumerate(near):
+        send(pack_src.at[0], packs.at[at], pack_ss.at[n_y + n], pack_rs.at[at], to)
+    for n, to in enumerate(sec_peers):
+        send(proj_hbm.at[0, 0], projs.at[sec], w_ss.at[1, n], w_rs.at[1, sec], to)
     loads[4].wait()
     loads[5].wait()
     gc_src[...] = jnp.zeros_like(gc_src)
     gc_src[0:1, :] = gain_in[0].astype(F32)
     gc_src[1:2, 0:heads] = coef_in[0].astype(F32)
     gcs[sec] = gc_src[...]
-
-    pl.semaphore_wait(barrier, len(partners))
-    send(code_src, code_got, code_ss, code_rs, across[0])
-    for n, to in enumerate(near + across):
-        r = 0 if n < len(near) else 1
-        send(pack_src.at[r], packs.at[at], pack_ss.at[n], pack_rs.at[at], to)
     for n, to in enumerate(sec_peers):
         send(gc_src, gcs.at[sec], w_ss.at[0, n], w_rs.at[0, sec], to)
-        send(proj_hbm.at[0, 0], projs.at[sec], w_ss.at[1, n], w_rs.at[1, sec], to)
+    for n, to in enumerate(sec_peers):
         send(outw_hbm.at[0, 0], outs.at[sec], w_ss.at[2, n], w_rs.at[2, sec], to)
+    code_own[...] = nbr_in[zh] + jnp.where(mask_in[zh] != 0, 0, unused)
 
     iota_hi = lax.broadcasted_iota(jnp.int32, (8, blk), 0)
     iota_lo = lax.broadcasted_iota(jnp.int32, (blk, blk), 0)
     none = jnp.zeros((8, blk), F32)
 
     def count(code_ref, r):
-        per = 16
-
-        def group(g, carry):
-            code = code_ref[pl.ds(pl.multiple_of(g * per, per), per), :]
-            hi = lax.shift_right_logical(code, 7)
-            lo = jnp.bitwise_and(code, blk - 1)
-            for i in range(0, per, 2):
-                left = [
-                    jnp.where(iota_hi == hi[i + e : i + e + 1, :], 1.0, 0.0).astype(F32)
+        code = code_ref[...]
+        hi = lax.shift_right_logical(code, 7)
+        lo = jnp.bitwise_and(code, blk - 1)
+        for i in range(0, blk, 2):
+            left = [
+                jnp.where(iota_hi == hi[i + e : i + e + 1, :], 1.0, 0.0).astype(F32)
+                for e in (0, 1)
+            ]
+            lhs = jnp.concatenate(
+                [
+                    jnp.concatenate([left[0], none], axis=1),
+                    jnp.concatenate([none, left[1]], axis=1),
+                ],
+                axis=0,
+            ).astype(BF16)
+            rhs = jnp.concatenate(
+                [
+                    jnp.where(iota_lo == lo[i + e : i + e + 1, :], 1.0, 0.0).astype(BF16)
                     for e in (0, 1)
-                ]
-                lhs = jnp.concatenate(
-                    [
-                        jnp.concatenate([left[0], none], axis=1),
-                        jnp.concatenate([none, left[1]], axis=1),
-                    ],
-                    axis=0,
-                ).astype(BF16)
-                rhs = jnp.concatenate(
-                    [
-                        jnp.where(iota_lo == lo[i + e : i + e + 1, :], 1.0, 0.0).astype(BF16)
-                        for e in (0, 1)
-                    ],
-                    axis=1,
-                )
-                both = lax.dot_general(lhs, rhs, NT, preferred_element_type=F32)
-                counts[pl.ds(pl.multiple_of((r * blk + g * per + i) * 8, 16), 16), :] = both
-            return carry
-
-        lax.fori_loop(0, blk // per, group, 0)
+                ],
+                axis=1,
+            )
+            both = lax.dot_general(lhs, rhs, NT, preferred_element_type=F32)
+            first_row = (r * blk + i) * 8
+            counts[first_row : first_row + 16, :] = both
 
     count(code_own, 0)
 
-    for y2 in ring:
-        got(packs.at[2 * y2 + zh], pack_rs.at[2 * y2 + zh])
-    for y2 in [y] + ring:
-        got(packs.at[2 * y2 + other], pack_rs.at[2 * y2 + other])
-
-    own_cols = [jnp.transpose(packs[2 * y + sides[r]]) for r in range(2)]
-
-    def pair_half(r):
-        for kb in range(n_atoms):
+    near_blocks = [2 * y2 + zh for y2 in [y] + ring]
+    far_blocks = [2 * y2 + other for y2 in [y] + ring]
+
+    def pair_half(r, cols, blocks):
+        for kb in blocks:
             pj = packs[kb]
             dist = jnp.zeros((blk, blk), F32)
             for d in range(3):
-                delta = pj[d : d + 1, :] - own_cols[r][:, d : d + 1]
+                delta = pj[d : d + 1, :] - cols[:, d : d + 1]
                 dist = dist + delta * delta
             cnt = counts[pl.ds(r * blk * 8 + kb, blk, stride=8), :]
             half_pair[r, kb] = 0.5 * cnt / (1.0 + 0.125 * dist)
 
-    pair_half(0)
-
     def normed(hf, gain):
         return (hf * lax.rsqrt(jnp.mean(hf * hf, -1, keepdims=True) + 1e-06) * gain).astype(BF16)
 
@@ -227,11 +220,13 @@
     def queries(x, layer, r):
         heads_apart(jnp.dot(x, projs[layer, :, 0:width], preferred_element_type=F32), r)
 
-    def keys(x, layer, kb):
+    def keys(x, layer, blocks):
         n_kv = width if layer == n_section - 1 else 2 * width
-        kv[layer % 2, kb, :, 0:n_kv] = jnp.dot(
+        out = jnp.dot(
             x, projs[layer, :, width : width + n_kv], preferred_element_type=F32
         ).astype(BF16)
+        for n, kb in enumerate(blocks):
+            kv[layer % 2, kb, :, 0:n_kv] = out[n * blk : (n + 1) * blk]
 
     def weights_ready(layer):
         @pl.when(sec != layer)
@@ -251,12 +246,14 @@
     def onehot(columns):
         return jnp.where(iota_type == columns[:, 3:4], 1.0, 0.0).astype(BF16)
 
-    for kb in range(n_atoms):
-        kv[0, kb] = jnp.dot(
-            onehot(jnp.transpose(packs[kb])), qkv_table[:, width:], preferred_element_type=F32
-        ).astype(BF16)
-    for r in range(2):
-        which = onehot(own_cols[r])
+    def first_keys(blocks):
+        for kb in blocks:
+            kv[0, kb] = jnp.dot(
+                onehot(jnp.transpose(packs[kb])), qkv_table[:, width:], preferred_element_type=F32
+            ).astype(BF16)
+
+    def first_rows(cols, r):
+        which = onehot(cols)
         hs[r] = jnp.dot(which, table[0], preferred_element_type=F32).astype(BF16)
         heads_apart(jnp.dot(which, qkv_table[:, 0:width], preferred_element_type=F32), r)
 
@@ -302,50 +299,62 @@
         mine = 2 * y + sides[r]
         xs[layer, mine] = x
         part = xs.at[layer, mine]
-        for n, to in enumerate(near):
+        for n, to in reversed(list(enumerate(near))):
             send(part, part, x_ss.at[layer, r, n], x_rs.at[layer, mine], to)
-        queries(x, layer + 1, r)
-        keys(x, layer + 1, mine)
-
-    def arrived(layer, y2, r):
-        kb = 2 * y2 + sides[r]
-        got(xs.at[layer - 1, kb], x_rs.at[layer - 1, kb])
-        keys(xs[layer - 1, kb], layer, kb)
-
-    own_pair = (2 * y + zh, 2 * y + other)
-    first_halves = [2 * y2 + zh for y2 in ring]
-    second_halves = [2 * y2 + other for y2 in ring]
-    rest = first_halves + second_halves
-    groups = [own_pair] + [tuple(rest[i : i + 2]) for i in range(0, len(rest), 2)]
-
-    for n, g in enumerate(groups):
-        unit(0, 0, g, n == 0)
+
+    def prepare(layer):
+        own = [xs[layer, 2 * y + sides[r]] for r in range(2)]
+        for r in range(2):
+            queries(own[r], layer + 1, r)
+        keys(jnp.concatenate(own, axis=0), layer + 1, [2 * y + zh, 2 * y + other])
+
+    def arrived(layer, r):
+        blocks = [2 * y2 + sides[r] for y2 in ring]
+        for kb in blocks:
+            got(xs.at[layer - 1, kb], x_rs.at[layer - 1, kb])
+        keys(jnp.concatenate([xs[layer - 1, kb] for kb in blocks], axis=0), layer, blocks)
+
+    for y2 in ring:
+        got(packs.at[2 * y2 + zh], pack_rs.at[2 * y2 + zh])
+    cols_own = jnp.transpose(packs[at])
+    pair_half(0, cols_own, near_blocks)
+    first_keys(near_blocks)
+    first_rows(cols_own, 0)
+    unit(0, 0, near_blocks, True)
+    for kb in far_blocks:
+        got(packs.at[kb], pack_rs.at[kb])
+    cols_far = jnp.transpose(packs[2 * y + other])
+    own_cols = [cols_own, cols_far]
+    pair_half(0, cols_own, far_blocks)
+    first_keys(far_blocks)
+    first_rows(cols_far, 1)
+    unit(0, 0, far_blocks, False)
     weights_ready(1)
     finish(0, 0)
     got(code_got, code_rs)
     count(code_got, 1)
-    pair_half(1)
-    for n, g in enumerate(groups):
-        unit(0, 1, g, n == 0)
+    pair_half(1, cols_far, near_blocks + far_blocks)
+    unit(0, 1, near_blocks, True)
+    unit(0, 1, far_blocks, False)
     finish(0, 1)
+    prepare(0)
 
     for layer in range(1, n_section):
         last = layer == n_section - 1
         for r in range(2):
-            unit(layer, r, groups[0], True)
-        for y2 in ring:
-            arrived(layer, y2, 0)
+            unit(layer, r, [2 * y + zh, 2 * y + other], True)
+        arrived(layer, 0)
         for r in range(2):
-            unit(layer, r, groups[1], False)
+            unit(layer, r, near_blocks[1:], False)
         if not last:
             weights_ready(layer + 1)
-        for y2 in ring:
-            arrived(layer, y2, 1)
+        arrived(layer, 1)
         for r in range(2):
-            for g in groups[2:]:
-                unit(layer, r, g, False)
+            unit(layer, r, far_blocks[1:], False)
             if not last:
                 finish(layer, r)
+        if not last:
+            prepare(layer)
 
     coef_all = jnp.zeros((1, 1), F32)
     for layer in range(n_section):
@@ -387,28 +396,36 @@
     d_all[at] = jnp.where(row < 3, mean_far, jnp.where(row == 3, dev[1], top))
     for n, to in enumerate(near + across):
         send(d_all.at[at], d_all.at[at], d_ss.at[n], d_rs.at[at], to)
-    result[zh] = jnp.where(row < 3, mean, jnp.where(row == 3, dev[0], 0.0))
     for y2 in ring:
         got(d_all.at[2 * y2 + zh], d_rs.at[2 * y2 + zh])
     for y2 in [y] + ring:
         got(d_all.at[2 * y2 + other], d_rs.at[2 * y2 + other])
-    result[other] = d_all[2 * y + other]
+    far = d_all[2 * y + other]
+    first = zh == 0
+    dev_out[0:1, :] = jnp.where(first, dev[0], far[3:4, :])
+    dev_out[1:2, :] = jnp.where(first, far[3:4, :], dev[0])
+    for d in range(3):
+        mean_out[d, 0:1, :] = jnp.where(first, mean[d : d + 1, :], far[d : d + 1, :])
+        mean_out[d, 1:2, :] = jnp.where(first, far[d : d + 1, :], mean[d : d + 1, :])
     for z in range(2):
         best = d_all[z]
         for y2 in range(1, n_y):
             best = jnp.maximum(best, d_all[2 * y2 + z])
-        result[z, 4:5, :] = best[4:5, :]
+        max_out[z] = jnp.max(best[4:5, :])
 
     for copy in sent:
         copy.wait_send()
 
 
-def finish_outputs(result, dev_out, max_out, mean_out):
-    for z in range(2):
-        for d in range(3):
-            mean_out[d, z : z + 1, :] = result[z, d : d + 1, :]
-        dev_out[z : z + 1, :] = result[z, 3:4, :]
-        max_out[z] = jnp.max(result[z, 4:5, :])
+def hand_on(dev_in, max_in, mean_in, dev_out, max_out, mean_out, sem):
+    copies = [
+        pltpu.make_async_copy(a, b, sem.at[n])
+        for n, (a, b) in enumerate([(dev_in, dev_out), (max_in, max_out), (mean_in, mean_out)])
+    ]
+    for c in copies:
+        c.start()
+    for c in copies:
+        c.wait()
 
 
 def shards(
@@ -476,11 +493,20 @@
         dma((n_atoms,)),
     ]
     own_frames = frames // n_section
-    result = pl.pallas_call(
+    results = (
+        jax.ShapeDtypeStruct((own_frames, blk), F32),
+        jax.ShapeDtypeStruct((own_frames,), F32),
+        jax.ShapeDtypeStruct((3, own_frames, blk), F32),
+    )
+    made = pl.pallas_call(
         functools.partial(kernel, dims),
-        out_shape=jax.ShapeDtypeStruct((own_frames, 8, blk), F32),
+        out_shape=results,
         in_specs=[pl.BlockSpec(memory_space=pltpu.HBM)] * 9,
-        out_specs=pl.BlockSpec(memory_space=pltpu.VMEM),
+        out_specs=(
+            pl.BlockSpec(memory_space=pltpu.VMEM),
+            pl.BlockSpec(memory_space=pltpu.SMEM),
+            pl.BlockSpec(memory_space=pltpu.VMEM),
+        ),
         scratch_shapes=scratch,
         compiler_params=pltpu.CompilerParams(
             collective_id=0, has_side_effects=True, vmem_limit_bytes=56 * 1024 * 1024
@@ -498,20 +524,13 @@
         force_coef,
     )
     atom_dev, max_dev, mean_force = pl.pallas_call(
-        finish_outputs,
-        out_shape=(
-            jax.ShapeDtypeStruct((own_frames, blk), F32),
-            jax.ShapeDtypeStruct((own_frames,), F32),
-            jax.ShapeDtypeStruct((3, own_frames, blk), F32),
-        ),
-        in_specs=[pl.BlockSpec(memory_space=pltpu.VMEM)],
-        out_specs=(
-            pl.BlockSpec(memory_space=pltpu.VMEM),
-            pl.BlockSpec(memory_space=pltpu.SMEM),
-            pl.BlockSpec(memory_space=pltpu.VMEM),
-        ),
+        hand_on,
+        out_shape=results,
+        in_specs=[pl.BlockSpec(memory_space=pl.ANY)] * 3,
+        out_specs=(pl.BlockSpec(memory_space=pl.ANY),) * 3,
+        scratch_shapes=[dma((3,))],
         name="outputs",
-    )(result)
+    )(*made)
     return (atom_dev, max_dev, jnp.transpose(mean_force, (1, 0, 2)))
 
 

time: 51.3 us -> 50.2 us (0.979)
  the two profiles are of different devices: /device:TPU:1 before, /device:TPU:4 now
where the time goes in v3:
time: 50.2 us; the launch traced here: 49.4 us
  Pallas kernels  48.8 us (97%)
  between operations  0.64 us (1%)
    pallas_call x1, Pallas kernels, shards(): pl.pallas_call(functools.partial(kernel, dims), out_shape=results, in_spe...  47.5 us
    pallas_call x1, Pallas kernels, shards(): pl.pallas_call(hand_on, out_shape=results, in_specs=[pl.BlockSpec(memory_...  1.27 us

profile of v3, /device:TPU:4, one launch (start us, length us, event | category | flops | bytes accessed | tf_op | source)
XLA Modules:
  0.0 49.4 jit_solution(14772570418870758530)
XLA Ops:
  0.6 47.5 %committee.1 = (f32[2,128]{1,0:T(2,128)}, f32[2]{0:T(128)}, f32[3,2,128]{2,1,0:T(2,128)}) custom-call(f32[3,8,128]{2,1,0:T(8,128)} %bitcast.2, s32[8,128]{1,0:T(8,128)} %types_hbm.1, s32[8,128,128]{2,1,0:T(8,128)} %nbr_hbm.1, s32[8,128,128]{2,1,0:T(8,128)} %mask_hbm.1, bf16[1,128,128]{2,1,0:T(8,128)(2,1)} %table_hbm.1, bf16[1,1,128]{2,1,0:T(2,128)(2,1)} %gain_hbm.1, ...), custom_call_target="tpu_custom_call" | custom-call | tf_op jit(solution)/shard_map/committee/pallas_call | solution.py:501
  48.2 1.3 %outputs.1 = (f32[2,128]{1,0:T(2,128)}, f32[2]{0:T(128)}, f32[3,2,128]{2,1,0:T(2,128)}) custom-call(f32[2,128]{1,0:T(2,128)} %get-tuple-element.9.dev_in, f32[2]{0:T(128)} %get-tuple-element.10.max_in, f32[3,2,128]{2,1,0:T(2,128)} %get-tuple-element.11.mean_in), custom_call_target="tpu_custom_call" | custom-call | tf_op jit(solution)/shard_map/outputs/pallas_call | solution.py:526

commit v4 on v3

--- a/solution.py
+++ b/solution.py
@@ -53,6 +53,7 @@
     hs,
     f_all,
     d_all,
+    pulled,
     in_sem,
     pack_ss,
     pack_rs,
@@ -89,9 +90,18 @@
     mates = [(me + k) % n_member for k in range(1, n_member)]
 
     barrier = pltpu.get_barrier_semaphore()
-    partners = across + near + sec_peers + [{"member": m2} for m2 in mates]
-    for device in partners:
-        pl.semaphore_signal(barrier, inc=1, device_id=device, device_id_type=pl.DeviceIdType.MESH)
+    far_mates = [(me + k) % n_member for k in range(n_member)]
+    partners = across[1:] + [{"member": m2, "atoms": 2 * y + other} for m2 in far_mates]
+    partners = partners + near + sec_peers + [{"member": m2} for m2 in mates]
+    n_far = n_y - 1 + n_member
+
+    def greet(devices):
+        for device in devices:
+            pl.semaphore_signal(
+                barrier, inc=1, device_id=device, device_id_type=pl.DeviceIdType.MESH
+            )
+
+    greet(partners[:n_far])
 
     frames2 = pl.ds(2 * sec, 2)
     loads = [
@@ -107,6 +117,7 @@
     ]
     for c in loads:
         c.start()
+    greet(partners[n_far:])
 
     def remote(src, dst, ss, rs, device):
         return pltpu.make_async_remote_copy(
@@ -124,6 +135,10 @@
         copy = remote(*what)
         copy.start()
         sent.append(copy)
+
+    def all_left():
+        while sent:
+            sent.pop(0).wait_send()
 
     def got(dst, rs):
         remote(dst, dst, x_ss.at[0, 0, 0], rs, sec_peers[0]).wait_recv()
@@ -141,6 +156,30 @@
     for n, to in enumerate(across):
         send(pack_src.at[1], packs.at[at], pack_ss.at[n], pack_rs.at[at], to)
 
+    loads[4].wait()
+    loads[5].wait()
+    gc_src[...] = jnp.zeros_like(gc_src)
+    gc_src[0:1, :] = gain_in[0].astype(F32)
+    gc_src[1:2, 0:heads] = coef_in[0].astype(F32)
+    gcs[sec] = gc_src[...]
+    shares = []
+    for a, b, what in (
+        (proj_hbm.at[0, 0], projs.at[sec], 1),
+        (gc_src, gcs.at[sec], 0),
+        (outw_hbm.at[0, 0], outs.at[sec], 2),
+    ):
+        for n, to in enumerate(sec_peers):
+            shares.append(remote(a, b, w_ss.at[what, n], w_rs.at[what, sec], to))
+    sent.extend(shares)
+
+    def share(when):
+        @pl.when(when)
+        def _():
+            for copy in shares:
+                copy.start()
+
+    share(sec == 0)
+
     loads[2].wait()
     loads[3].wait()
     unused = n_atoms * blk
@@ -148,18 +187,6 @@
     send(code_src, code_got, code_ss, code_rs, across[0])
     for n, to in enumerate(near):
         send(pack_src.at[0], packs.at[at], pack_ss.at[n_y + n], pack_rs.at[at], to)
-    for n, to in enumerate(sec_peers):
-        send(proj_hbm.at[0, 0], projs.at[sec], w_ss.at[1, n], w_rs.at[1, sec], to)
-    loads[4].wait()
-    loads[5].wait()
-    gc_src[...] = jnp.zeros_like(gc_src)
-    gc_src[0:1, :] = gain_in[0].astype(F32)
-    gc_src[1:2, 0:heads] = coef_in[0].astype(F32)
-    gcs[sec] = gc_src[...]
-    for n, to in enumerate(sec_peers):
-        send(gc_src, gcs.at[sec], w_ss.at[0, n], w_rs.at[0, sec], to)
-    for n, to in enumerate(sec_peers):
-        send(outw_hbm.at[0, 0], outs.at[sec], w_ss.at[2, n], w_rs.at[2, sec], to)
     code_own[...] = nbr_in[zh] + jnp.where(mask_in[zh] != 0, 0, unused)
 
     iota_hi = lax.broadcasted_iota(jnp.int32, (8, blk), 0)
@@ -194,6 +221,7 @@
             counts[first_row : first_row + 16, :] = both
 
     count(code_own, 0)
+    share(sec != 0)
 
     near_blocks = [2 * y2 + zh for y2 in [y] + ring]
     far_blocks = [2 * y2 + other for y2 in [y] + ring]
@@ -321,6 +349,8 @@
     first_keys(near_blocks)
     first_rows(cols_own, 0)
     unit(0, 0, near_blocks, True)
+    got(code_got, code_rs)
+    count(code_got, 1)
     for kb in far_blocks:
         got(packs.at[kb], pack_rs.at[kb])
     cols_far = jnp.transpose(packs[2 * y + other])
@@ -331,13 +361,19 @@
     unit(0, 0, far_blocks, False)
     weights_ready(1)
     finish(0, 0)
-    got(code_got, code_rs)
-    count(code_got, 1)
     pair_half(1, cols_far, near_blocks + far_blocks)
     unit(0, 1, near_blocks, True)
     unit(0, 1, far_blocks, False)
     finish(0, 1)
     prepare(0)
+
+    def pull(r, blocks, parts):
+        for kb in blocks:
+            pj = packs[kb]
+            w = half_pair[r, kb] * (coef_sum[r, kb] + coef_all)
+            for d in range(3):
+                parts[d] = parts[d] + w * (pj[d : d + 1, :] - own_cols[r][:, d : d + 1])
+        return parts
 
     for layer in range(1, n_section):
         last = layer == n_section - 1
@@ -348,6 +384,14 @@
             unit(layer, r, near_blocks[1:], False)
         if not last:
             weights_ready(layer + 1)
+        else:
+            coef_all = jnp.zeros((1, 1), F32)
+            for b in range(n_section):
+                coef_all = coef_all + jnp.sum(gcs[b, 1:2, :], axis=1, keepdims=True)
+            for r in range(2):
+                parts = pull(r, near_blocks + far_blocks[:1], [jnp.zeros((blk, blk), F32)] * 3)
+                for d in range(3):
+                    pulled[r, d] = parts[d]
         arrived(layer, 1)
         for r in range(2):
             unit(layer, r, far_blocks[1:], False)
@@ -356,65 +400,74 @@
         if not last:
             prepare(layer)
 
-    coef_all = jnp.zeros((1, 1), F32)
-    for layer in range(n_section):
-        coef_all = coef_all + jnp.sum(gcs[layer, 1:2, :], axis=1, keepdims=True)
     column = lax.broadcasted_iota(jnp.int32, (blk, 8), 1)
     tile = jnp.zeros((blk, 8), F32)
     for r in range(2):
-        parts = [jnp.zeros((blk, blk), F32)] * 3
-        for kb in range(n_atoms):
-            pj = packs[kb]
-            pull = half_pair[r, kb] * (coef_sum[r, kb] + coef_all)
-            for d in range(3):
-                parts[d] = parts[d] + pull * (pj[d : d + 1, :] - own_cols[r][:, d : d + 1])
+        parts = pull(r, far_blocks[1:], [pulled[r, d] for d in range(3)])
         for d in range(3):
-            tile = jnp.where(
-                column == 4 * r + d, jnp.sum(parts[d], axis=1, keepdims=True), tile
-            )
-    f_all[me] = jnp.transpose(tile) * (1.0 / slots)
+            tile = jnp.where(column == 4 * r + d, jnp.sum(parts[d], axis=1, keepdims=True), tile)
+    f_all[zh, me] = jnp.transpose(tile) * (1.0 / slots)
+    before = list(sent)
+    sent.clear()
+    mine = f_all.at[zh, me]
+    for n, m2 in enumerate(far_mates):
+        to = {"member": m2, "atoms": 2 * y + other}
+        send(mine, mine, f_ss.at[n_member + n], f_rs.at[zh, me], to)
     for n, m2 in enumerate(mates):
-        send(f_all.at[me], f_all.at[me], f_ss.at[n], f_rs.at[me], {"member": m2})
+        send(mine, mine, f_ss.at[n], f_rs.at[zh, me], {"member": m2})
+
+    for copy in before:
+        copy.wait_send()
+    row = lax.broadcasted_iota(jnp.int32, (8, blk), 0)
+
+    def statistics(side):
+        total = f_all[side, 0]
+        for m in range(1, n_member):
+            total = total + f_all[side, m]
+        mean = total * (1.0 / n_member)
+        square = jnp.zeros((8, blk), F32)
+        for m in range(n_member):
+            centered = f_all[side, m] - mean
+            square = square + centered * centered
+        dev = [
+            jnp.sqrt(jnp.sum(square[4 * r : 4 * r + 4], axis=0, keepdims=True) * (1.0 / n_member))
+            for r in range(2)
+        ]
+        return mean, dev
+
     for m2 in mates:
-        got(f_all.at[m2], f_rs.at[m2])
-
-    total = f_all[0]
-    for m in range(1, n_member):
-        total = total + f_all[m]
-    mean = total * (1.0 / n_member)
-    square = jnp.zeros((8, blk), F32)
-    for m in range(n_member):
-        centered = f_all[m] - mean
-        square = square + centered * centered
-    dev = [
-        jnp.sqrt(jnp.sum(square[4 * r : 4 * r + 4], axis=0, keepdims=True) * (1.0 / n_member))
-        for r in range(2)
-    ]
-    row = lax.broadcasted_iota(jnp.int32, (8, blk), 0)
-    top = jnp.where(row == 4, jnp.maximum(dev[0], dev[1]), 0.0)
-    mean_far = jnp.concatenate([mean[4:8], mean[0:4]], axis=0)
-    d_all[at] = jnp.where(row < 3, mean_far, jnp.where(row == 3, dev[1], top))
-    for n, to in enumerate(near + across):
-        send(d_all.at[at], d_all.at[at], d_ss.at[n], d_rs.at[at], to)
+        got(f_all.at[zh, m2], f_rs.at[zh, m2])
+    mean, dev = statistics(zh)
+    for m2 in far_mates:
+        got(f_all.at[other, m2], f_rs.at[other, m2])
+    mean_far, dev_far = statistics(other)
+    mean_far = mean_far[4:8]
+    d_all[y] = jnp.where(
+        row == 0,
+        jnp.maximum(dev[0], dev[1]),
+        jnp.where(row == 1, jnp.maximum(dev_far[0], dev_far[1]), 0.0),
+    )
+    for n, to in enumerate(near):
+        send(d_all.at[y], d_all.at[y], d_ss.at[n], d_rs.at[y], to)
+    for copy in sent[: -len(near)]:
+        copy.wait_send()
+    del sent[: -len(near)]
+    first = zh == 0
+    dev_out[0:1, :] = jnp.where(first, dev[0], dev_far[1])
+    dev_out[1:2, :] = jnp.where(first, dev_far[1], dev[0])
+    for d in range(3):
+        here, there = mean[d : d + 1, :], mean_far[d : d + 1, :]
+        mean_out[d, 0:1, :] = jnp.where(first, here, there)
+        mean_out[d, 1:2, :] = jnp.where(first, there, here)
     for y2 in ring:
-        got(d_all.at[2 * y2 + zh], d_rs.at[2 * y2 + zh])
-    for y2 in [y] + ring:
-        got(d_all.at[2 * y2 + other], d_rs.at[2 * y2 + other])
-    far = d_all[2 * y + other]
-    first = zh == 0
-    dev_out[0:1, :] = jnp.where(first, dev[0], far[3:4, :])
-    dev_out[1:2, :] = jnp.where(first, far[3:4, :], dev[0])
-    for d in range(3):
-        mean_out[d, 0:1, :] = jnp.where(first, mean[d : d + 1, :], far[d : d + 1, :])
-        mean_out[d, 1:2, :] = jnp.where(first, far[d : d + 1, :], mean[d : d + 1, :])
-    for z in range(2):
-        best = d_all[z]
-        for y2 in range(1, n_y):
-            best = jnp.maximum(best, d_all[2 * y2 + z])
-        max_out[z] = jnp.max(best[4:5, :])
-
-    for copy in sent:
-        copy.wait_send()
+        got(d_all.at[y2], d_rs.at[y2])
+    best = d_all[0]
+    for y2 in range(1, n_y):
+        best = jnp.maximum(best, d_all[y2])
+    max_out[zh] = jnp.max(best[0:1, :])
+    max_out[other] = jnp.max(best[1:2, :])
+
+    all_left()
 
 
 def hand_on(dev_in, max_in, mean_in, dev_out, max_out, mean_out, sem):
@@ -476,8 +529,9 @@
         vmem((2, heads * blk, width), BF16),
         vmem((2, heads * blk, width), F32),
         vmem((2, blk, width), BF16),
-        vmem((n_member, 8, blk), F32),
-        vmem((n_atoms, 8, blk), F32),
+        vmem((2, n_member, 8, blk), F32),
+        vmem((n_y, 8, blk), F32),
+        vmem((2, 3, blk, blk), F32),
         dma((9,)),
         dma((n_atoms,)),
         dma((n_atoms,)),
@@ -487,10 +541,10 @@
         dma((3, n_section)),
         dma((n_section - 1, 2, n_y)),
         dma((n_section - 1, n_atoms)),
-        dma((n_member,)),
-        dma((n_member,)),
-        dma((n_atoms,)),
-        dma((n_atoms,)),
+        dma((2 * n_member,)),
+        dma((2, n_member)),
+        dma((n_y,)),
+        dma((n_y,)),
     ]
     own_frames = frames // n_section
     results = (

time: 50.2 us -> 49.2 us (0.980); the launches traced: 49.4 us -> 49 us
  no operation moved by 1% of the time
where the time goes in v4:
time: 49.2 us; the launch traced here: 49 us
  Pallas kernels  48.4 us (98%)
  between operations  0.64 us (1%)
    pallas_call x1, Pallas kernels, shards(): pl.pallas_call(functools.partial(kernel, dims), out_shape=results, in_spe...  47.1 us
    pallas_call x1, Pallas kernels, shards(): pl.pallas_call(hand_on, out_shape=results, in_specs=[pl.BlockSpec(memory_...  1.27 us

profile of v4, /device:TPU:4, one launch (start us, length us, event | category | flops | bytes accessed | tf_op | source)
XLA Modules:
  0.0 49.0 jit_solution(7506547763816917648)
XLA Ops:
  0.6 47.1 %committee.1 = (f32[2,128]{1,0:T(2,128)}, f32[2]{0:T(128)}, f32[3,2,128]{2,1,0:T(2,128)}) custom-call(f32[3,8,128]{2,1,0:T(8,128)} %bitcast.2, s32[8,128]{1,0:T(8,128)} %types_hbm.1, s32[8,128,128]{2,1,0:T(8,128)} %nbr_hbm.1, s32[8,128,128]{2,1,0:T(8,128)} %mask_hbm.1, bf16[1,128,128]{2,1,0:T(8,128)(2,1)} %table_hbm.1, bf16[1,1,128]{2,1,0:T(2,128)(2,1)} %gain_hbm.1, ...), custom_call_target="tpu_custom_call" | custom-call | tf_op jit(solution)/shard_map/committee/pallas_call | solution.py:555
  47.7 1.3 %outputs.1 = (f32[2,128]{1,0:T(2,128)}, f32[2]{0:T(128)}, f32[3,2,128]{2,1,0:T(2,128)}) custom-call(f32[2,128]{1,0:T(2,128)} %get-tuple-element.9.dev_in, f32[2]{0:T(128)} %get-tuple-element.10.max_in, f32[3,2,128]{2,1,0:T(2,128)} %get-tuple-element.11.mean_in), custom_call_target="tpu_custom_call" | custom-call | tf_op jit(solution)/shard_map/outputs/pallas_call | solution.py:580

commit v5 on v4

--- a/solution.py
+++ b/solution.py
@@ -156,17 +156,17 @@
     for n, to in enumerate(across):
         send(pack_src.at[1], packs.at[at], pack_ss.at[n], pack_rs.at[at], to)
 
-    loads[4].wait()
-    loads[5].wait()
+    for c in loads[4:8]:
+        c.wait()
     gc_src[...] = jnp.zeros_like(gc_src)
     gc_src[0:1, :] = gain_in[0].astype(F32)
     gc_src[1:2, 0:heads] = coef_in[0].astype(F32)
     gcs[sec] = gc_src[...]
     shares = []
     for a, b, what in (
-        (proj_hbm.at[0, 0], projs.at[sec], 1),
+        (projs.at[sec], projs.at[sec], 1),
         (gc_src, gcs.at[sec], 0),
-        (outw_hbm.at[0, 0], outs.at[sec], 2),
+        (outs.at[sec], outs.at[sec], 2),
     ):
         for n, to in enumerate(sec_peers):
             shares.append(remote(a, b, w_ss.at[what, n], w_rs.at[what, sec], to))
@@ -263,8 +263,7 @@
             got(projs.at[layer], w_rs.at[1, layer])
             got(outs.at[layer], w_rs.at[2, layer])
 
-    for c in loads[6:]:
-        c.wait()
+    loads[8].wait()
     weights_ready(0)
 
     x_table = normed(table[0].astype(F32), gcs[0, 0:1, :])

time: 49.2 us -> 48.9 us (level)
  no operation moved by 1% of the time
where the time goes in v5:
time: 48.9 us; the launch traced here: 48.8 us
  Pallas kernels  48.1 us (98%)
  between operations  0.64 us (1%)
    pallas_call x1, Pallas kernels, shards(): pl.pallas_call(functools.partial(kernel, dims), out_shape=results, in_spe...  46.9 us
    pallas_call x1, Pallas kernels, shards(): pl.pallas_call(hand_on, out_shape=results, in_specs=[pl.BlockSpec(memory_...  1.27 us

profile of v5, /device:TPU:4, one launch (start us, length us, event | category | flops | bytes accessed | tf_op | source)
XLA Modules:
  0.0 48.8 jit_solution(8517117209787125651)
XLA Ops:
  0.6 46.9 %committee.1 = (f32[2,128]{1,0:T(2,128)}, f32[2]{0:T(128)}, f32[3,2,128]{2,1,0:T(2,128)}) custom-call(f32[3,8,128]{2,1,0:T(8,128)} %bitcast.2, s32[8,128]{1,0:T(8,128)} %types_hbm.1, s32[8,128,128]{2,1,0:T(8,128)} %nbr_hbm.1, s32[8,128,128]{2,1,0:T(8,128)} %mask_hbm.1, bf16[1,128,128]{2,1,0:T(8,128)(2,1)} %table_hbm.1, bf16[1,1,128]{2,1,0:T(2,128)(2,1)} %gain_hbm.1, ...), custom_call_target="tpu_custom_call" | custom-call | tf_op jit(solution)/shard_map/committee/pallas_call | solution.py:554
  47.5 1.3 %outputs.1 = (f32[2,128]{1,0:T(2,128)}, f32[2]{0:T(128)}, f32[3,2,128]{2,1,0:T(2,128)}) custom-call(f32[2,128]{1,0:T(2,128)} %get-tuple-element.9.dev_in, f32[2]{0:T(128)} %get-tuple-element.10.max_in, f32[3,2,128]{2,1,0:T(2,128)} %get-tuple-element.11.mean_in), custom_call_target="tpu_custom_call" | custom-call | tf_op jit(solution)/shard_map/outputs/pallas_call | solution.py:579

commit v6 on v5

--- a/solution.py
+++ b/solution.py
@@ -164,8 +164,8 @@
     gcs[sec] = gc_src[...]
     shares = []
     for a, b, what in (
+        (gc_src, gcs.at[sec], 0),
         (projs.at[sec], projs.at[sec], 1),
-        (gc_src, gcs.at[sec], 0),
         (outs.at[sec], outs.at[sec], 2),
     ):
         for n, to in enumerate(sec_peers):
@@ -256,15 +256,24 @@
         for n, kb in enumerate(blocks):
             kv[layer % 2, kb, :, 0:n_kv] = out[n * blk : (n + 1) * blk]
 
-    def weights_ready(layer):
+    def gain_ready(layer):
         @pl.when(sec != layer)
         def _():
             got(gcs.at[layer], w_rs.at[0, layer])
+
+    def proj_ready(layer):
+        @pl.when(sec != layer)
+        def _():
             got(projs.at[layer], w_rs.at[1, layer])
+
+    def out_ready(layer):
+        @pl.when(sec != layer)
+        def _():
             got(outs.at[layer], w_rs.at[2, layer])
 
     loads[8].wait()
-    weights_ready(0)
+    gain_ready(0)
+    proj_ready(0)
 
     x_table = normed(table[0].astype(F32), gcs[0, 0:1, :])
     qkv_table = jnp.dot(x_table, projs[0], preferred_element_type=F32).astype(BF16)
@@ -330,6 +339,7 @@
             send(part, part, x_ss.at[layer, r, n], x_rs.at[layer, mine], to)
 
     def prepare(layer):
+        proj_ready(layer + 1)
         own = [xs[layer, 2 * y + sides[r]] for r in range(2)]
         for r in range(2):
             queries(own[r], layer + 1, r)
@@ -358,7 +368,8 @@
     first_keys(far_blocks)
     first_rows(cols_far, 1)
     unit(0, 0, far_blocks, False)
-    weights_ready(1)
+    out_ready(0)
+    gain_ready(1)
     finish(0, 0)
     pair_half(1, cols_far, near_blocks + far_blocks)
     unit(0, 1, near_blocks, True)
@@ -382,7 +393,8 @@
         for r in range(2):
             unit(layer, r, near_blocks[1:], False)
         if not last:
-            weights_ready(layer + 1)
+            out_ready(layer)
+            gain_ready(layer + 1)
         else:
             coef_all = jnp.zeros((1, 1), F32)
             for b in range(n_section):
@@ -399,6 +411,7 @@
         if not last:
             prepare(layer)
 
+    out_ready(n_section - 1)
     column = lax.broadcasted_iota(jnp.int32, (blk, 8), 1)
     tile = jnp.zeros((blk, 8), F32)
     for r in range(2):

time: 48.9 us -> 48.2 us (0.986)
  Pallas kernels: 48.1 us -> 47.4 us
    pallas_call x1, Pallas kernels: 46.9 us -> 46.2 us  [shards(): pl.pallas_call(functools.partial(kernel, dims), out_shape=results, in_spe...]
where the time goes in v6:
time: 48.2 us; the launch traced here: 48.1 us
  Pallas kernels  47.4 us (98%)
  between operations  0.64 us (1%)
    pallas_call x1, Pallas kernels, shards(): pl.pallas_call(functools.partial(kernel, dims), out_shape=results, in_spe...  46.2 us
    pallas_call x1, Pallas kernels, shards(): pl.pallas_call(hand_on, out_shape=results, in_specs=[pl.BlockSpec(memory_...  1.27 us

profile of v6, /device:TPU:4, one launch (start us, length us, event | category | flops | bytes accessed | tf_op | source)
XLA Modules:
  0.0 48.1 jit_solution(12218535035000324154)
XLA Ops:
  0.6 46.2 %committee.1 = (f32[2,128]{1,0:T(2,128)}, f32[2]{0:T(128)}, f32[3,2,128]{2,1,0:T(2,128)}) custom-call(f32[3,8,128]{2,1,0:T(8,128)} %bitcast.2, s32[8,128]{1,0:T(8,128)} %types_hbm.1, s32[8,128,128]{2,1,0:T(8,128)} %nbr_hbm.1, s32[8,128,128]{2,1,0:T(8,128)} %mask_hbm.1, bf16[1,128,128]{2,1,0:T(8,128)(2,1)} %table_hbm.1, bf16[1,1,128]{2,1,0:T(2,128)(2,1)} %gain_hbm.1, ...), custom_call_target="tpu_custom_call" | custom-call | tf_op jit(solution)/shard_map/committee/pallas_call | solution.py:567
  46.8 1.3 %outputs.1 = (f32[2,128]{1,0:T(2,128)}, f32[2]{0:T(128)}, f32[3,2,128]{2,1,0:T(2,128)}) custom-call(f32[2,128]{1,0:T(2,128)} %get-tuple-element.9.dev_in, f32[2]{0:T(128)} %get-tuple-element.10.max_in, f32[3,2,128]{2,1,0:T(2,128)} %get-tuple-element.11.mean_in), custom_call_target="tpu_custom_call" | custom-call | tf_op jit(solution)/shard_map/outputs/pallas_call | solution.py:592
